TPU v7x, 32 devices: a whole 2x2x4 slice. The times are simulated.
32 devices in a mesh: groups: 2 (over y), row: 4 (over z), col: 2 (over x), chan: 2 (over core).
Axes of the slice: x: 2, y: 2, z: 4, core: 2. Of those that a mesh axis runs over, the one named last changes fastest.
Arguments:
- pair_input: bfloat16 [512, 256, 128], P(('groups', 'row'), ('col', 'chan')), parts along dimension 0, may hold values from -6 to 6
- alignment_features: bfloat16 [128, 512, 64], P('row', ('groups', 'col', 'chan')), parts along dimension 1, may hold values from -6 to 6
- alignment_mask: int32 [128, 512], P('row', ('groups', 'col', 'chan')), parts along dimension 1, may hold values from 0 to 1
- token_valid: int32 [512], P('groups'), parts along dimension 0, may hold values from 0 to 1, as said below
- left_weight: bfloat16 [64, 32], replicated, may hold values from -0.75 to 0.75
- right_weight: bfloat16 [64, 32], replicated, may hold values from -0.75 to 0.75
- output_weight: bfloat16 [1024, 128], replicated, may hold values from -1.75 to 1.75
- gate_weight: bfloat16 [128, 512], replicated, may hold values from -0.5 to 0.5
- up_weight: bfloat16 [128, 512], replicated, may hold values from -0.5 to 0.5
- down_weight: bfloat16 [512, 128], replicated, may hold values from -0.25 to 0.25
- kernel_weight: bfloat16 [3, 3, 128, 128], replicated, may hold values from -0.1875 to 0.1875
Outputs:
- pair_out: bfloat16 [512, 256, 128], P(('groups', 'row'), ('col', 'chan')), parts along dimension 0
There are 2 independent parts, one for each index of `groups`. A program takes and returns all parts, laid end to end along the dimension named above; an argument that names none is the same for every part. Nothing has to cross between parts.
Inputs may be any that keep to these rules, and one draw needn't show every extreme that they name: `token_valid`: the ones come first.
All inputs are finite; a program needn't handle non-finite values.
Results may differ from a plain program's by a relative error of at most 0.014.
Values may be sent and summed in bfloat16 or wider, within the bound.
A program may use at most 64 MiB of HBM per device.

v0:
```python
import math

import jax
import jax.numpy as jnp
from jax import lax
from jax.sharding import PartitionSpec as P

epsilon = 1e-05


def with_halo(value, sides, width):
    for axis, dim in sides:
        size, length = (lax.axis_size(axis), value.shape[dim])
        up = [(i, (i + 1) % size) for i in range(size - 1)]
        down = [(j, i) for i, j in up]
        last = lax.slice_in_dim(value, length - width, length, axis=dim)
        initial = lax.slice_in_dim(value, 0, width, axis=dim)
        before = lax.ppermute(last, axis, up)
        after = lax.ppermute(initial, axis, down)
        value = jnp.concatenate([before, value, after], axis=dim)
    return value


def transition(pair_rows, gate_weight, up_weight, down_weight):
    values = pair_rows.astype(jnp.float32)
    centre = jnp.mean(values, axis=-1, keepdims=True)
    spread = jnp.mean(jnp.square(values - centre), axis=-1, keepdims=True)
    normed = ((values - centre) * lax.rsqrt(spread + epsilon)).astype(jnp.bfloat16)
    gate_act = jnp.dot(normed, gate_weight, preferred_element_type=jnp.float32)
    up_act = jnp.dot(normed, up_weight, preferred_element_type=jnp.float32)
    hidden = (jax.nn.silu(gate_act) * up_act).astype(jnp.bfloat16)
    return (values + jnp.dot(hidden, down_weight, preferred_element_type=jnp.float32)).astype(
        jnp.bfloat16
    )


def on_device(
    pair_input,
    alignment_features,
    alignment_mask,
    token_valid,
    left_weight,
    right_weight,
    output_weight,
    gate_weight,
    up_weight,
    down_weight,
    kernel_weight,
):
    rows_dev, cols_dev, channels = pair_input.shape
    local_row_count, local_token_count, alignment_width = alignment_features.shape
    opm_width = left_weight.shape[1]
    row_count = lax.axis_size("row")
    col_count = lax.axis_size(("col", "chan"))
    fold_ratio = row_count // col_count
    row_index = lax.axis_index("row")
    col_index = lax.axis_index(("col", "chan"))
    halved_mask = alignment_mask.astype(jnp.bfloat16)
    column_mask = alignment_mask.reshape(local_row_count * local_token_count, 1).astype(jnp.float32)
    alignment_flat = alignment_features.reshape(
        local_row_count * local_token_count, alignment_width
    )
    left_local = (
        jnp.dot(alignment_flat, left_weight, preferred_element_type=jnp.float32) * column_mask
    ).astype(jnp.bfloat16)
    left_local = left_local.reshape(local_row_count, local_token_count, opm_width)
    right_local = (
        jnp.dot(alignment_flat, right_weight, preferred_element_type=jnp.float32) * column_mask
    ).astype(jnp.bfloat16)
    right_local = right_local.reshape(local_row_count, local_token_count, opm_width)
    right_projected, right_mask = (
        lax.all_gather(right_local, "row", axis=0, tiled=True),
        lax.all_gather(halved_mask, "row", axis=0, tiled=True),
    )
    wide_left, wide_mask = (
        lax.all_gather(left_local, ("col", "chan"), axis=1, tiled=True),
        lax.all_gather(halved_mask, ("col", "chan"), axis=1, tiled=True),
    )
    left_projected, left_mask = (
        lax.all_to_all(wide_left, "row", split_axis=1, concat_axis=0, tiled=True),
        lax.all_to_all(wide_mask, "row", split_axis=1, concat_axis=0, tiled=True),
    )
    depth_all = left_projected.shape[0]
    counts = lax.dot_general(
        left_mask, right_mask, (((0,), (0,)), ((), ())), preferred_element_type=jnp.float32
    )
    right_flat = right_projected.reshape(depth_all, cols_dev * opm_width)
    strip_rows = math.gcd(16, rows_dev)

    def outer_rows(first_row):
        left_part = lax.dynamic_slice_in_dim(left_projected, first_row, strip_rows, 1).reshape(
            depth_all, strip_rows * opm_width
        )
        products = lax.dot_general(
            left_part, right_flat, (((0,), (0,)), ((), ())), preferred_element_type=jnp.float32
        )
        products = products.reshape(strip_rows, opm_width, cols_dev, opm_width).transpose(
            0, 2, 1, 3
        )
        products = products.reshape(strip_rows * cols_dev, opm_width * opm_width).astype(
            jnp.bfloat16
        )
        update = jnp.dot(products, output_weight, preferred_element_type=jnp.float32).reshape(
            strip_rows, cols_dev, channels
        )
        pair_count = lax.dynamic_slice_in_dim(counts, first_row, strip_rows, 0)
        update = update / jnp.maximum(pair_count, 1.0)[:, :, None]
        base_pair = lax.dynamic_slice_in_dim(pair_input, first_row, strip_rows, 0).astype(
            jnp.float32
        )
        return (base_pair + update).astype(jnp.bfloat16)

    starts = jnp.arange(rows_dev // strip_rows, dtype=jnp.int32) * strip_rows
    pair_one = lax.map(outer_rows, starts).reshape(rows_dev, cols_dev, channels)

    def apply_transition(pair_tile):
        total_rows = rows_dev * cols_dev
        slab_size = math.gcd(1024, total_rows)
        pair_slabs = pair_tile.reshape(total_rows // slab_size, slab_size, channels)

        def one_slab(pair_slab):
            return transition(pair_slab, gate_weight, up_weight, down_weight)

        return lax.map(one_slab, pair_slabs).reshape(rows_dev, cols_dev, channels)

    share_rows = rows_dev // col_count
    second_step = lax.all_to_all(
        lax.all_to_all(pair_one, ("col", "chan"), split_axis=0, concat_axis=1, tiled=True),
        "row",
        split_axis=1,
        concat_axis=0,
        tiled=True,
    )
    flipped = jnp.swapaxes(second_step, 0, 1)
    third_step = lax.all_to_all(flipped, ("col", "chan"), split_axis=1, concat_axis=1, tiled=True)
    arranged = third_step.reshape(rows_dev, col_count, fold_ratio, share_rows, channels).transpose(
        0, 2, 1, 3, 4
    )
    mirrored_one = arranged.reshape(rows_dev, cols_dev, channels)
    pair_two = apply_transition(pair_one)
    pair_mirror = apply_transition(mirrored_one)
    pad_real = token_valid.astype(jnp.float32)
    pad_rows = lax.dynamic_slice_in_dim(pad_real, row_index * rows_dev, rows_dev)
    pad_cols = lax.dynamic_slice_in_dim(pad_real, col_index * cols_dev, cols_dev)
    symmetric = (pair_two.astype(jnp.float32) + pair_mirror.astype(jnp.float32)) * 0.5
    masked = (symmetric * pad_rows[:, None, None] * pad_cols[None, :, None]).astype(jnp.bfloat16)
    padded = with_halo(masked, (("row", 0), (("col", "chan"), 1)), 1)
    summed = jnp.zeros((rows_dev * cols_dev, channels), jnp.float32)
    for shift_row in range(3):
        for shift_col in range(3):
            shifted = padded[
                shift_row : shift_row + rows_dev, shift_col : shift_col + cols_dev
            ].reshape(rows_dev * cols_dev, channels)
            summed = summed + jnp.dot(
                shifted, kernel_weight[shift_row, shift_col], preferred_element_type=jnp.float32
            )
    result = symmetric.reshape(rows_dev * cols_dev, channels) + summed
    return result.astype(jnp.bfloat16).reshape(rows_dev, cols_dev, channels)


def solution(mesh):
    placed = (
        P(("groups", "row"), ("col", "chan"), None),
        P("row", ("groups", "col", "chan"), None),
        P("row", ("groups", "col", "chan")),
        P("groups"),
        P(),
        P(),
        P(),
        P(),
        P(),
        P(),
        P(),
    )
    return jax.shard_map(
        on_device,
        mesh=mesh,
        in_specs=placed,
        out_specs=P(("groups", "row"), ("col", "chan"), None),
        check_vma=False,
    )
```

profile of v0, /device:TPU:9, one launch (start us, length us, event | category | flops | bytes accessed | tf_op | source)
XLA Modules:
  0.0 239.9 jit_solution(9252353414318188215)
XLA Ops:
  0.8 5.7 %all-gather = bf16[4,64,32]{1,2,0:T(8,128)(2,1)S(1)} all-gather(bf16[1,64,32]{1,2,0:T(8,128)(2,1)S(1)} %bitcast.246), channel_id=1, replica_groups=mesh['groups'=2,'row'=4,'col'=2,'chan'=2] {'col','chan'}, dimensions={0}, use_global_device_ids=true | all-gather | bytes 20480 | tf_op jit(solution)/shard_map/all_gather | solution.py:77
  7.4 4.8 %all-to-all-start.1 = ((bf16[4,2,1024]{2,1,0:T(2,128)(2,1)}), bf16[4,2,1024]{2,1,0:T(2,128)(2,1)S(1)}, u32[]{:S(2)}, u32[]{:S(2)}) async-start(bf16[4,2,1024]{2,1,0:T(2,128)(2,1)} %reshape.147), calls=%async_computation.1 | async-start | bytes 32768 | tf_op jit(solution)/shard_map/all_to_all | solution.py:81
  14.4 16.3 %all_gather.12 = bf16[32,256,32]{2,0,1:T(8,128)(2,1)S(1)} all-gather(bf16[32,64,32]{2,0,1:T(8,128)(2,1)S(1)} %copy.48), channel_id=1, replica_groups=mesh['groups'=2,'row'=4,'col'=2,'chan'=2] {'col','chan'}, dimensions={1}, use_global_device_ids=true | all-gather | bytes 655360 | tf_op jit(solution)/shard_map/all_gather | solution.py:76
  30.7 2.9 %reshape.145 = bf16[4,2,32768]{2,1,0:T(2,128)(2,1)} reshape(bf16[256,32,32]{2,1,0:T(8,128)(2,1)S(1)} %bitcast.227) | data formatting | bytes 1048576
  33.6 4.5 %all-to-all-start = ((bf16[4,2,32768]{2,1,0:T(2,128)(2,1)}), bf16[4,2,32768]{2,1,0:T(2,128)(2,1)S(1)}, u32[]{:S(2)}, u32[]{:S(2)}) async-start(bf16[4,2,32768]{2,1,0:T(2,128)(2,1)} %reshape.145), calls=%async_computation | async-start | bytes 1048576 | tf_op jit(solution)/shard_map/all_to_all | solution.py:80
  38.8 28.8 %all_gather.13 = bf16[128,64,32]{1,2,0:T(8,128)(2,1)S(1)} all-gather(bf16[32,64,32]{1,2,0:T(8,128)(2,1)S(1)} %copy.51), channel_id=1, replica_groups=mesh['groups'=2,'row'=4,'col'=2,'chan'=2] {'row'}, dimensions={0}, use_global_device_ids=true | all-gather | bytes 655360 | tf_op jit(solution)/shard_map/all_gather | solution.py:72
  67.6 1.5 copy.52
  69.2 8.5 %all_gather.15 = bf16[128,64]{1,0:T(8,128)(2,1)S(1)} all-gather(bf16[32,64]{1,0:T(8,128)(2,1)S(1)} %get-tuple-element.203), channel_id=1, replica_groups=mesh['groups'=2,'row'=4,'col'=2,'chan'=2] {'row'}, dimensions={0}, use_global_device_ids=true | all-gather | bytes 20480 | tf_op jit(solution)/shard_map/all_gather | solution.py:73
  77.9 2.4 %reshape.146 = bf16[256,32,32]{2,1,0:T(8,128)(2,1)} reshape(bf16[4,2,32768]{2,1,0:T(2,128)(2,1)S(1)} %all-to-all-done) | data formatting | bytes 1048576
  80.3 3.5 %copy.63 = bf16[32,4,64,32]{2,1,3,0:T(4,128)(2,1)S(1)} copy(bf16[32,4,64,32]{3,0,2,1:T(8,128)(2,1)} %bitcast.228) | data formatting | bytes 1048576 | tf_op jit(solution)/shard_map/all_to_all | solution.py:80
  85.0 2.8 %copy.55 = bf16[128,64,32]{0,2,1:T(8,128)(2,1)S(1)} copy(bf16[128,64,32]{1,2,0:T(8,128)(2,1)} %bitcast.240) | data formatting | bytes 1048576 | tf_op jit(solution)/shard_map/while | solution.py:114
  87.8 31.8 %while.30 = (s32[]{:T(128)}, bf16[4,16,64,128]{3,2,1,0:T(8,128)(2,1)S(1)}, s32[4]{0:T(128)S(1)}, bf16[64,64,128]{2,1,0:T(8,128)(2,1)}, bf16[128,64,32]{0,2,1:T(8...) while((s32[]{:T(128)}, ...), condition=%wide.region_1.2_spmd, body=%wide.region_0.1_spmd.sunk | while | flops 538444800 | bytes 11944115 | solution.py:114
  90.4 1.3 convert_bitcast_fusion.4
  91.7 1.8 copy.74
  93.5 2.3 fusion.143
  98.3 1.3 convert_bitcast_fusion.4
  99.6 1.8 copy.74
  101.4 2.3 fusion.143
  106.3 1.3 convert_bitcast_fusion.4
  107.6 1.8 copy.74
  109.4 2.3 fusion.143
  114.2 1.3 convert_bitcast_fusion.4
  115.5 1.8 copy.74
  117.3 2.3 fusion.143
  119.7 22.1 %all_to_all.78 = bf16[64,64,128]{2,1,0:T(8,128)(2,1)S(1)} all-to-all(bf16[64,64,128]{2,1,0:T(8,128)(2,1)S(1)} %bitcast.222), channel_id=1, replica_groups=mesh['groups'=2,'row'=4,'col'=2,'chan'=2] {'col','chan'}, dimensions={0} | all-to-all | bytes 2097152 | tf_op jit(solution)/shard_map/all_to_all | solution.py:128
  141.9 1.6 copy.57
  143.6 4.5 %all-to-all-start.3 = ((bf16[16,256,128]{2,0,1:T(8,128)(2,1)}), bf16[16,256,128]{2,0,1:T(8,128)(2,1)S(1)}, u32[]{:S(2)}, u32[]{:S(2)}) async-start(bf16[16,256,128]{2,0,1:T(8,128)(2,1)} %copy.57), calls=%async_computation.3 | async-start | bytes 2097152 | tf_op jit(solution)/shard_map/all_to_all | solution.py:127
  148.5 21.1 %all-to-all-done.3 = bf16[16,256,128]{2,0,1:T(8,128)(2,1)S(1)} async-done(((bf16[16,256,128]{2,0,1:T(8,128)(2,1)}), bf16[16,256,128]{2,0,1:T(8,128)(2,1)S(1)}, u32[]{:S(2)}, u32[]{:S(2)}) %all-to-all-start.3) | async-done | bytes 1048608 | tf_op jit(solution)/shard_map/all_to_all | solution.py:127
  170.9 6.5 %all-to-all-start.4 = ((bf16[64,64,128]{2,0,1:T(8,128)(2,1)}), bf16[64,64,128]{2,0,1:T(8,128)(2,1)}, u32[]{:S(2)}, u32[]{:S(2)}) async-start(bf16[64,64,128]{2,0,1:T(8,128)(2,1)} %bitcast.36), calls=%async_computation.4 | async-start | bytes 2097152 | tf_op jit(solution)/shard_map/all_to_all | solution.py:135
  178.5 14.7 %while.31 = (s32[]{:T(128)}, bf16[4,1024,128]{2,1,0:T(8,128)(2,1)}, bf16[4,1024,128]{2,1,0:T(8,128)(2,1)S(1)}, bf16[128,512]{1,0:T(8,128)(2,1)S(1)}, bf16[128,51...) while((s32[]{:T(128)}, bf16[4,1024,128]{2,1,0:T(8,128)(2,1)}, ...), condition=%wide.region_5.6_spmd, body=%wide.region_2.5_spmd.sunk | while | flops 408028160 | bytes 6206561 | solution.py:124
  179.5 2.7 %fusion.151 = bf16[4,1024,128]{2,1,0:T(8,128)(2,1)} fusion(bf16[4,1024,128]{2,1,0:T(8,128)(2,1)} %get-tuple-element.395, s32[]{:T(128)S(6)} %copy.92, bf16[512,128]{1,0:T(8,128)(2,1)} %get-tuple-element.406, f32[1024,512]{1,0:T(8,128)S(1)} %fusion.150, bf16[128,512]{1,0:T(8,128)(2,1)S(1)} %get-tuple-element.404, f32[1024]{0:T(1024)S(1)} %add_rsqrt_fusion.4, ...), kind=kOutput, calls=%fused_computation.18.clone.1 | convolution fusion | flops 272498688 | bytes 3154944 | tf_op jit(solution)/shard_map/while/body/eval_jaxpr/dot_general | solution.py:32
  183.2 2.6 %fusion.151 = bf16[4,1024,128]{2,1,0:T(8,128)(2,1)} fusion(bf16[4,1024,128]{2,1,0:T(8,128)(2,1)} %get-tuple-element.395, s32[]{:T(128)S(6)} %copy.92, bf16[512,128]{1,0:T(8,128)(2,1)} %get-tuple-element.406, f32[1024,512]{1,0:T(8,128)S(1)} %fusion.150, bf16[128,512]{1,0:T(8,128)(2,1)S(1)} %get-tuple-element.404, f32[1024]{0:T(1024)S(1)} %add_rsqrt_fusion.4, ...), kind=kOutput, calls=%fused_computation.18.clone.1 | convolution fusion | flops 272498688 | bytes 3154944 | tf_op jit(solution)/shard_map/while/body/eval_jaxpr/dot_general | solution.py:32
  186.9 2.6 %fusion.151 = bf16[4,1024,128]{2,1,0:T(8,128)(2,1)} fusion(bf16[4,1024,128]{2,1,0:T(8,128)(2,1)} %get-tuple-element.395, s32[]{:T(128)S(6)} %copy.92, bf16[512,128]{1,0:T(8,128)(2,1)} %get-tuple-element.406, f32[1024,512]{1,0:T(8,128)S(1)} %fusion.150, bf16[128,512]{1,0:T(8,128)(2,1)S(1)} %get-tuple-element.404, f32[1024]{0:T(1024)S(1)} %add_rsqrt_fusion.4, ...), kind=kOutput, calls=%fused_computation.18.clone.1 | convolution fusion | flops 272498688 | bytes 3154944 | tf_op jit(solution)/shard_map/while/body/eval_jaxpr/dot_general | solution.py:32
  190.6 2.7 %fusion.151 = bf16[4,1024,128]{2,1,0:T(8,128)(2,1)} fusion(bf16[4,1024,128]{2,1,0:T(8,128)(2,1)} %get-tuple-element.395, s32[]{:T(128)S(6)} %copy.92, bf16[512,128]{1,0:T(8,128)(2,1)} %get-tuple-element.406, f32[1024,512]{1,0:T(8,128)S(1)} %fusion.150, bf16[128,512]{1,0:T(8,128)(2,1)S(1)} %get-tuple-element.404, f32[1024]{0:T(1024)S(1)} %add_rsqrt_fusion.4, ...), kind=kOutput, calls=%fused_computation.18.clone.1 | convolution fusion | flops 272498688 | bytes 3154944 | tf_op jit(solution)/shard_map/while/body/eval_jaxpr/dot_general | solution.py:32
  193.2 1.9 copy.60
  196.2 14.7 %while.32 = (s32[]{:T(128)}, bf16[4,1024,128]{2,1,0:T(8,128)(2,1)}, bf16[4,1024,128]{2,1,0:T(8,128)(2,1)S(1)}, bf16[128,512]{1,0:T(8,128)(2,1)S(1)}, bf16[128,51...) while((s32[]{:T(128)}, bf16[4,1024,128]{2,1,0:T(8,128)(2,1)}, ...), condition=%wide.region_9.10_spmd, body=%wide.region_6.9_spmd.sunk | while | flops 408028160 | bytes 6206561 | solution.py:124
  197.3 2.6 %fusion.159 = bf16[4,1024,128]{2,1,0:T(8,128)(2,1)} fusion(bf16[4,1024,128]{2,1,0:T(8,128)(2,1)} %get-tuple-element.374, s32[]{:T(128)S(6)} %copy.86, bf16[512,128]{1,0:T(8,128)(2,1)} %get-tuple-element.385, f32[1024,512]{1,0:T(8,128)S(1)} %fusion.158, bf16[128,512]{1,0:T(8,128)(2,1)S(1)} %get-tuple-element.383, f32[1024]{0:T(1024)S(1)} %add_rsqrt_fusion.5, ...), kind=kOutput, calls=%fused_computation.44.clone.1 | convolution fusion | flops 272498688 | bytes 3154944 | tf_op jit(solution)/shard_map/while/body/eval_jaxpr/dot_general | solution.py:32
  200.9 2.6 %fusion.159 = bf16[4,1024,128]{2,1,0:T(8,128)(2,1)} fusion(bf16[4,1024,128]{2,1,0:T(8,128)(2,1)} %get-tuple-element.374, s32[]{:T(128)S(6)} %copy.86, bf16[512,128]{1,0:T(8,128)(2,1)} %get-tuple-element.385, f32[1024,512]{1,0:T(8,128)S(1)} %fusion.158, bf16[128,512]{1,0:T(8,128)(2,1)S(1)} %get-tuple-element.383, f32[1024]{0:T(1024)S(1)} %add_rsqrt_fusion.5, ...), kind=kOutput, calls=%fused_computation.44.clone.1 | convolution fusion | flops 272498688 | bytes 3154944 | tf_op jit(solution)/shard_map/while/body/eval_jaxpr/dot_general | solution.py:32
  204.6 2.6 %fusion.159 = bf16[4,1024,128]{2,1,0:T(8,128)(2,1)} fusion(bf16[4,1024,128]{2,1,0:T(8,128)(2,1)} %get-tuple-element.374, s32[]{:T(128)S(6)} %copy.86, bf16[512,128]{1,0:T(8,128)(2,1)} %get-tuple-element.385, f32[1024,512]{1,0:T(8,128)S(1)} %fusion.158, bf16[128,512]{1,0:T(8,128)(2,1)S(1)} %get-tuple-element.383, f32[1024]{0:T(1024)S(1)} %add_rsqrt_fusion.5, ...), kind=kOutput, calls=%fused_computation.44.clone.1 | convolution fusion | flops 272498688 | bytes 3154944 | tf_op jit(solution)/shard_map/while/body/eval_jaxpr/dot_general | solution.py:32
  208.3 2.6 %fusion.159 = bf16[4,1024,128]{2,1,0:T(8,128)(2,1)} fusion(bf16[4,1024,128]{2,1,0:T(8,128)(2,1)} %get-tuple-element.374, s32[]{:T(128)S(6)} %copy.86, bf16[512,128]{1,0:T(8,128)(2,1)} %get-tuple-element.385, f32[1024,512]{1,0:T(8,128)S(1)} %fusion.158, bf16[128,512]{1,0:T(8,128)(2,1)S(1)} %get-tuple-element.383, f32[1024]{0:T(1024)S(1)} %add_rsqrt_fusion.5, ...), kind=kOutput, calls=%fused_computation.44.clone.1 | convolution fusion | flops 272498688 | bytes 3154944 | tf_op jit(solution)/shard_map/while/body/eval_jaxpr/dot_general | solution.py:32
  210.9 2.1 multiply_convert_fusion.2
  213.6 4.9 %collective-permute-start.1 = (bf16[1,64,128]{2,1,0:T(8,128)(2,1)S(1)}, bf16[1,64,128]{2,1,0:T(8,128)(2,1)S(1)}, u32[]{:S(2)}, u32[]{:S(2)}) collective-permute-start(bf16[1,64,128]{2,1,0:T(8,128)(2,1)S(1)} %get-tuple-element.202), channel_id=1, source_target_pairs={{4,0},{8,4},{12,8},{5,1},{9,5},{13,9},{6,2},{10,6},{14,10},{7,3},{... | collective-permute-start | bytes 49160 | tf_op jit(solution)/shard_map/ppermute | solution.py:19
  218.6 2.1 collective-permute-start
  220.6 2.5 %collective-permute-done = bf16[1,64,128]{2,1,0:T(8,128)(2,1)S(1)} collective-permute-done((bf16[1,64,128]{2,1,0:T(8,128)(2,1)S(1)}, bf16[1,64,128]{2,1,0:T(8,128)(2,1)S(1)}, u32[]{:S(2)}, u32[]{:S(2)}) %collective-permute-start) | collective-permute-done | bytes 16416 | tf_op jit(solution)/shard_map/ppermute | solution.py:18
  223.2 5.0 %collective-permute-start.2 = (bf16[66,1,128]{2,1,0:T(2,128)(2,1)S(1)}, bf16[66,1,128]{2,1,0:T(2,128)(2,1)S(1)}, u32[]{:S(2)}, u32[]{:S(2)}) collective-permute-start(bf16[66,1,128]{2,1,0:T(2,128)(2,1)S(1)} %get-tuple-element.197), channel_id=1, source_target_pairs={{0,1},{1,2},{2,3},{4,5},{5,6},{6,7},{8,9},{9,10},{10,11},{12,13},{... | collective-permute-start | bytes 50696 | tf_op jit(solution)/shard_map/ppermute | solution.py:18
  228.2 2.1 collective-permute-start.3
  231.0 2.5 %collective-permute-done.3 = bf16[66,1,128]{2,1,0:T(2,128)(2,1)S(1)} collective-permute-done((bf16[66,1,128]{2,1,0:T(2,128)(2,1)S(1)}, bf16[66,1,128]{2,1,0:T(2,128)(2,1)S(1)}, u32[]{:S(2)}, u32[]{:S(2)}) %collective-permute-start.3) | collective-permute-done | bytes 16928 | tf_op jit(solution)/shard_map/ppermute | solution.py:19
  238.5 1.4 fusion.68
  (112 shorter events, 26.5 us)
Async XLA Ops:
  0.0 12.2 %copy-start = (bf16[32,64,64]{2,1,0:T(8,128)(2,1)S(1)}, bf16[32,64,64]{2,1,0:T(8,128)(2,1)}, u32[]{:S(2)}) copy-start(bf16[32,64,64]{2,1,0:T(8,128)(2,1)} %param.18) | copy-start | bytes 786436
  7.4 26.2 %all-to-all-start.1 = ((bf16[4,2,1024]{2,1,0:T(2,128)(2,1)}), bf16[4,2,1024]{2,1,0:T(2,128)(2,1)S(1)}, u32[]{:S(2)}, u32[]{:S(2)}) async-start(bf16[4,2,1024]{2,1,0:T(2,128)(2,1)} %reshape.147), calls=%async_computation.1 | async-start | bytes 32768 | tf_op jit(solution)/shard_map/all_to_all | solution.py:81
  30.7 7.5 %copy-start.4 = (bf16[64,32]{0,1:T(8,128)(2,1)S(1)}, bf16[64,32]{0,1:T(8,128)(2,1)}, u32[]{:S(2)}) copy-start(bf16[64,32]{0,1:T(8,128)(2,1)} %param.22) | copy-start | bytes 12292
  33.6 44.3 %all-to-all-start = ((bf16[4,2,32768]{2,1,0:T(2,128)(2,1)}), bf16[4,2,32768]{2,1,0:T(2,128)(2,1)S(1)}, u32[]{:S(2)}, u32[]{:S(2)}) async-start(bf16[4,2,32768]{2,1,0:T(2,128)(2,1)} %reshape.145), calls=%async_computation | async-start | bytes 1048576 | tf_op jit(solution)/shard_map/all_to_all | solution.py:80
  83.8 4.0 %copy-start.6 = (bf16[1024,128]{1,0:T(8,128)(2,1)S(1)}, bf16[1024,128]{1,0:T(8,128)(2,1)}, u32[]{:S(2)}) copy-start(bf16[1024,128]{1,0:T(8,128)(2,1)} %param.23) | copy-start | bytes 786436
  141.9 6.2 %copy-start.5 = (s32[256]{0:T(256)S(1)}, s32[256]{0:T(256)}, u32[]{:S(2)}) copy-start(s32[256]{0:T(256)} %param.20) | copy-start | bytes 3076
  143.6 26.1 %all-to-all-start.3 = ((bf16[16,256,128]{2,0,1:T(8,128)(2,1)}), bf16[16,256,128]{2,0,1:T(8,128)(2,1)S(1)}, u32[]{:S(2)}, u32[]{:S(2)}) async-start(bf16[16,256,128]{2,0,1:T(8,128)(2,1)} %copy.57), calls=%async_computation.3 | async-start | bytes 2097152 | tf_op jit(solution)/shard_map/all_to_all | solution.py:127
  170.9 7.6 %copy-start.2 = (bf16[128,512]{1,0:T(8,128)(2,1)S(1)}, bf16[128,512]{1,0:T(8,128)(2,1)}, u32[]{:S(2)}) copy-start(bf16[128,512]{1,0:T(8,128)(2,1)} %param.25) | copy-start | bytes 393220
  170.9 7.6 %copy-start.7 = (bf16[128,512]{1,0:T(8,128)(2,1)S(1)}, bf16[128,512]{1,0:T(8,128)(2,1)}, u32[]{:S(2)}) copy-start(bf16[128,512]{1,0:T(8,128)(2,1)} %param.24) | copy-start | bytes 393220
  170.9 22.4 %all-to-all-start.4 = ((bf16[64,64,128]{2,0,1:T(8,128)(2,1)}), bf16[64,64,128]{2,0,1:T(8,128)(2,1)}, u32[]{:S(2)}, u32[]{:S(2)}) async-start(bf16[64,64,128]{2,0,1:T(8,128)(2,1)} %bitcast.36), calls=%async_computation.4 | async-start | bytes 2097152 | tf_op jit(solution)/shard_map/all_to_all | solution.py:135
  213.6 7.0 %collective-permute-start.1 = (bf16[1,64,128]{2,1,0:T(8,128)(2,1)S(1)}, bf16[1,64,128]{2,1,0:T(8,128)(2,1)S(1)}, u32[]{:S(2)}, u32[]{:S(2)}) collective-permute-start(bf16[1,64,128]{2,1,0:T(8,128)(2,1)S(1)} %get-tuple-element.202), channel_id=1, source_target_pairs={{4,0},{8,4},{12,8},{5,1},{9,5},{13,9},{6,2},{10,6},{14,10},{7,3},{... | collective-permute-start | bytes 49160 | tf_op jit(solution)/shard_map/ppermute | solution.py:19
  218.6 12.0 %copy-start.3 = (bf16[3,3,128,128]{3,2,1,0:T(8,128)(2,1)S(1)}, bf16[3,3,128,128]{3,2,1,0:T(8,128)(2,1)}, u32[]{:S(2)}) copy-start(bf16[3,3,128,128]{3,2,1,0:T(8,128)(2,1)} %param.27) | copy-start | bytes 884740
  218.6 4.6 %collective-permute-start = (bf16[1,64,128]{2,1,0:T(8,128)(2,1)S(1)}, bf16[1,64,128]{2,1,0:T(8,128)(2,1)S(1)}, u32[]{:S(2)}, u32[]{:S(2)}) collective-permute-start(bf16[1,64,128]{2,1,0:T(8,128)(2,1)S(1)} %get-tuple-element.201), channel_id=1, source_target_pairs={{0,4},{4,8},{8,12},{1,5},{5,9},{9,13},{2,6},{6,10},{10,14},{3,7},{... | collective-permute-start | bytes 49160 | tf_op jit(solution)/shard_map/ppermute | solution.py:18
  223.2 7.7 %collective-permute-start.2 = (bf16[66,1,128]{2,1,0:T(2,128)(2,1)S(1)}, bf16[66,1,128]{2,1,0:T(2,128)(2,1)S(1)}, u32[]{:S(2)}, u32[]{:S(2)}) collective-permute-start(bf16[66,1,128]{2,1,0:T(2,128)(2,1)S(1)} %get-tuple-element.197), channel_id=1, source_target_pairs={{0,1},{1,2},{2,3},{4,5},{5,6},{6,7},{8,9},{9,10},{10,11},{12,13},{... | collective-permute-start | bytes 50696 | tf_op jit(solution)/shard_map/ppermute | solution.py:18
  228.2 5.2 %collective-permute-start.3 = (bf16[66,1,128]{2,1,0:T(2,128)(2,1)S(1)}, bf16[66,1,128]{2,1,0:T(2,128)(2,1)S(1)}, u32[]{:S(2)}, u32[]{:S(2)}) collective-permute-start(bf16[66,1,128]{2,1,0:T(2,128)(2,1)S(1)} %get-tuple-element.198), channel_id=1, source_target_pairs={{1,0},{2,1},{3,2},{5,4},{6,5},{7,6},{9,8},{10,9},{11,10},{13,12},{... | collective-permute-start | bytes 50696 | tf_op jit(solution)/shard_map/ppermute | solution.py:19
  238.4 1.4 copy-start.1
where the time goes:
time: 241 us; the launch traced here: 240 us
  blocking collectives  81.4 us (34%)
  matrix products  45.7 us (19%)
  local copies, waits for them, and re-layouts  35 us (15%)
  starting transfers between devices  34.4 us (14%)
  waiting for transfers between devices  26.2 us (11%)
  other arithmetic  8.75 us (4%)
  loops' own time  8.13 us (3%)
    all_gather x1, blocking collectives, on_device(): lax.all_gather(right_local, 'row', axis=0, tiled=True)  28.8 us
    all_to_all x1, blocking collectives, on_device(): lax.all_to_all(pair_one, ('col', 'chan'), split_axis=0, concat_axis=1, ti...  22.1 us
    dot_general x8, matrix products, transition(): jnp.dot(hidden, down_weight, preferred_element_type=jnp.float32)  21.2 us
    all_to_all x1, waiting for transfers between devices, on_device(): lax.all_to_all(lax.all_to_all(pair_one, ('col', 'chan'), split_axis=0, co...  21.1 us
    all_gather x1, blocking collectives, on_device(): lax.all_gather(left_local, ('col', 'chan'), axis=1, tiled=True)  16.3 us
    dot_general x4, matrix products, outer_rows(): jnp.dot(products, output_weight, preferred_element_type=jnp.float32)  9.26 us
    all_gather x1, blocking collectives, on_device(): lax.all_gather(halved_mask, 'row', axis=0, tiled=True)  8.46 us
    another operation x1, loops' own time, on_device(): pair_one = lax.map(outer_rows, starts).reshape(rows_dev, cols_dev, channels)  7.94 us
  transfers between devices with their start and end apart: 8, of which 3 were waited for; matrix products, arithmetic and copies ran while one was open for 10% of the time, Pallas kernels for 0%

commit v1 on v0

v1 whole, which is shorter than its diff:
```python
import functools

import jax
import jax.numpy as jnp
from jax import lax
from jax.experimental import pallas as pl
from jax.experimental.pallas import tpu as pltpu
from jax.sharding import PartitionSpec as P

epsilon = 1e-05
F32, BF16 = jnp.float32, jnp.bfloat16
MESH = pl.DeviceIdType.MESH
AROUND = [(a, b) for a in (-1, 0, 1) for b in (-1, 0, 1) if (a, b) != (0, 0)]


def dot(a, b):
    return jnp.dot(a, b, preferred_element_type=F32)


def block_kernel(
    sizes,
    pair_ref,
    feat_ref,
    mask_ref,
    valid_ref,
    wl_ref,
    wr_ref,
    wo_ref,
    wg_ref,
    wu_ref,
    wd_ref,
    wk_ref,
    out_ref,
    lsend,
    lg,
    rg,
    rt,
    rq,
    lcat,
    wof,
    w4,
    zs,
    rexp,
    ones,
    two,
    mirror,
    mf,
    sym,
    wide,
    colf,
    hsend,
    hrecv,
    l1_send,
    l1_recv,
    l2_send,
    l2_recv,
    r_send,
    r_recv,
    m_send,
    m_recv,
    h_send,
    h_recv,
):
    rn, cn, chans, fold, rd, cd, ch, sl, tl, pw, cr = sizes
    row = lax.axis_index("row")
    col = lax.axis_index("col") * chans + lax.axis_index("chan")
    per = 128 // pw
    lgroups, rgroups = rd // per, cd // per
    depth = rn * sl
    steps = rd // cr
    cgroups = cr // per

    def at(r, c):
        return {"row": r, "col": c // chans, "chan": c % chans}

    def remote(src, dst, ssem, rsem, r, c):
        return pltpu.make_async_remote_copy(
            src_ref=src, dst_ref=dst, send_sem=ssem, recv_sem=rsem,
            device_id=at(r, c), device_id_type=MESH,
        )

    hrecv[...] = jnp.zeros_like(hrecv)
    barrier = pltpu.get_barrier_semaphore()

    def greet(n, carry):
        pl.semaphore_signal(barrier, inc=1, device_id=at(n // cn, n % cn), device_id_type=MESH)
        return carry

    lax.fori_loop(0, rn * cn, greet, 0)

    aw = wl_ref.shape[0]
    spread = (
        lax.broadcasted_iota(jnp.int32, (pw, 128), 1) % pw
        == lax.broadcasted_iota(jnp.int32, (pw, 128), 0)
    ).astype(F32).astype(BF16)
    own = (
        lax.broadcasted_iota(jnp.int32, (per * aw, 128), 0) // aw
        == lax.broadcasted_iota(jnp.int32, (per * aw, 128), 1) // pw
    )

    def block_weight(w):
        tiled = dot(w, spread)
        return jnp.where(own, jnp.concatenate([tiled] * per, axis=0), 0.0).astype(BF16)

    feats = feat_ref[...]
    left = dot(feats, block_weight(wl_ref[...])).reshape(tl // per, sl, 128).astype(BF16)
    right = dot(feats, block_weight(wr_ref[...])).reshape(tl // per, sl, 128).astype(BF16)
    mask = mask_ref[...].astype(F32).astype(BF16)
    for k in range(fold):
        lsend[k, 0:lgroups] = left[k * lgroups : (k + 1) * lgroups]
        lsend[k, lgroups] = jnp.zeros((sl, 128), BF16)
        lsend[k, lgroups, :, 0:rd] = mask[:, k * rd : (k + 1) * rd]
    rg[row, 0:rgroups] = right
    rg[row, rgroups] = jnp.zeros((sl, 128), BF16)
    rg[row, rgroups, :, 0:tl] = mask

    pl.semaphore_wait(barrier, rn * cn)

    for k in range(fold):
        to_row, to_col = col * fold + k, row % cn
        mine = jnp.logical_and(to_row == row, to_col == col)
        slot = row // cn

        @pl.when(mine)
        def _():
            pltpu.make_async_copy(lsend.at[k], lg.at[row], l1_recv.at[slot]).start()

        @pl.when(jnp.logical_not(mine))
        def _():
            remote(lsend.at[k], lg.at[row], l1_send.at[k], l1_recv.at[slot], to_row, to_col).start()

    for d in range(1, rn):
        remote(
            rg.at[row], rg.at[row], r_send.at[d - 1], r_recv.at[d - 1], (row + d) % rn, col
        ).start()

    wof[...] = wo_ref[...].astype(F32)
    w4[...] = jnp.zeros_like(w4)
    for q in range(pw):
        part = wof[pl.ds(q, pw, stride=pw), :].astype(BF16)
        for i in range(per):
            w4[q * 128 + i * pw : q * 128 + (i + 1) * pw, i * ch : (i + 1) * ch] = part

    for m in range(fold):
        slot = col + m * cn
        pltpu.make_async_copy(lg.at[slot], lg.at[slot], l1_recv.at[m]).wait()
        for d in range(1, cn):
            remote(
                lg.at[slot], lg.at[slot], l2_send.at[m, d - 1], l2_recv.at[m, d - 1],
                row, (col + d) % cn,
            ).start()

    for d in range(1, rn):
        slot = (row + rn - d) % rn
        pltpu.make_async_copy(rg.at[slot], rg.at[slot], r_recv.at[d - 1]).wait()
    for g in range(rgroups):
        slab = rg[:, g].astype(F32).reshape(depth, 128)
        rt[g * 128 : (g + 1) * 128, :] = slab.T
    for q in range(pw):
        rq[q * cd : (q + 1) * cd, :] = rt[pl.ds(q, cd, stride=pw), :].astype(BF16)

    for m in range(fold):
        for d in range(1, cn):
            slot = (col + cn - d) % cn + m * cn
            pltpu.make_async_copy(lg.at[slot], lg.at[slot], l2_recv.at[m, d - 1]).wait()
    for g in range(lgroups):
        slab = lg[:, g].astype(F32).reshape(depth, 128).astype(BF16)
        where = g % cgroups
        lcat[g // cgroups, :, where * 128 : (where + 1) * 128] = slab
    left_mask = lg[:, lgroups].astype(F32).reshape(depth, 128)
    right_mask = rg[:, rgroups].astype(F32).reshape(depth, 128)
    counts = dot(right_mask.T.astype(BF16), left_mask.astype(BF16))
    inverse = 1.0 / jnp.maximum(counts, 1.0)
    for i in range(rd):
        rexp[i] = jnp.broadcast_to(inverse[0:cd, i : i + 1], (cd, ch))

    qstep = min(8, pw)

    def to_mirror(step, k):
        src = two.at[pl.ds(step * cr, cr), pl.ds(k * rd, rd)]
        dst = mirror.at[pl.ds((row % fold) * rd + step * cr, cr)]
        return src, dst

    def one_step(step, carry):
        lpart = lcat[step]
        for q0 in range(0, pw, qstep):
            z = dot(rq[q0 * cd : (q0 + qstep) * cd, :], lpart).astype(BF16)
            for q in range(qstep):
                for g in range(cgroups):
                    zs[g * cd : (g + 1) * cd, (q0 + q) * 128 : (q0 + q + 1) * 128] = z[
                        q * cd : (q + 1) * cd, g * 128 : (g + 1) * 128
                    ]
        update = dot(zs[...], w4[...])
        for g in range(cgroups):
            for i in range(per):
                at_row = step * cr + g * per + i
                add = update[g * cd : (g + 1) * cd, i * ch : (i + 1) * ch] * rexp[at_row]
                ones[g * per + i] = (pair_ref[at_row].astype(F32) + add).astype(BF16)
        half = max(1, cr // 2)
        for h in range(0, cr, half):
            values = ones[h : h + half].reshape(half * cd, ch).astype(F32)
            centre = jnp.mean(values, axis=-1, keepdims=True)
            shifted = values - centre
            var = jnp.mean(jnp.square(shifted), axis=-1, keepdims=True)
            normed = (shifted * lax.rsqrt(var + epsilon)).astype(BF16)
            gate = dot(normed, wg_ref[...])
            up = dot(normed, wu_ref[...])
            hidden = (gate / (1.0 + jnp.exp(-gate)) * up).astype(BF16)
            result = (values + dot(hidden, wd_ref[...])).astype(BF16)
            two[pl.ds(step * cr + h, half)] = result.reshape(half, cd, ch)
        for k in range(fold):
            to_row, to_col = col * fold + k, row // fold
            mine = jnp.logical_and(to_row == row, to_col == col)
            src, dst = to_mirror(step, k)
            rsem = m_recv.at[row % fold, step]

            @pl.when(mine)
            def _():
                pltpu.make_async_copy(src, dst, rsem).start()

            @pl.when(jnp.logical_not(mine))
            def _():
                remote(src, dst, m_send.at[k, step], rsem, to_row, to_col).start()

        return carry

    lax.fori_loop(0, steps, one_step, 0)

    for step in range(steps):
        for k in range(fold):
            piece = mirror.at[pl.ds(k * rd + step * cr, cr)]
            pltpu.make_async_copy(piece, piece, m_recv.at[k, step]).wait()
            begin = k * rd + step * cr
            mf[begin * rd : (begin + cr) * rd, :] = (
                mirror[begin : begin + cr].astype(F32).reshape(cr * rd, ch)
            )

    valid_cols = valid_ref[pl.ds(pl.multiple_of(col * cd, 8), cd), :]

    def one_row(i, carry):
        half_sum = (two[i].astype(F32) + mf[pl.ds(i, cd, stride=rd), :]) * 0.5
        sym[i] = half_sum
        masked = half_sum * valid_cols * valid_ref[pl.ds(row * rd + i, 1), :]
        wide[i + 1, :, ch : 2 * ch] = masked.astype(BF16)
        colf[0, pl.ds(i, 1), :] = masked[0:1]
        colf[1, pl.ds(i, 1), :] = masked[cd - 1 : cd]
        return carry

    lax.fori_loop(0, rd, one_row, 0)

    for n, (a, b) in enumerate(AROUND):
        if b == 0:
            hsend[n, 0:cd] = wide[1 if a < 0 else rd, :, ch : 2 * ch]
        elif a == 0:
            hsend[n, 0:rd] = colf[0 if b < 0 else 1].astype(BF16)
        else:
            corner = colf[0 if b < 0 else 1, 0:1] if a < 0 else colf[0 if b < 0 else 1, rd - 1 : rd]
            hsend[n, 0:16] = jnp.broadcast_to(corner, (16, ch)).astype(BF16)

    def there(a, b):
        r, c = row + a, col + b
        return jnp.logical_and(
            jnp.logical_and(r >= 0, r < rn), jnp.logical_and(c >= 0, c < cn)
        )

    def lines(a, b):
        return cd if b == 0 else (rd if a == 0 else 16)

    for n, (a, b) in enumerate(AROUND):

        @pl.when(there(a, b))
        def _():
            size = lines(a, b)
            remote(
                hsend.at[n, pl.ds(0, size)], hrecv.at[n, pl.ds(0, size)], h_send.at[n],
                h_recv.at[n], row + a, col + b,
            ).start()

    for n, (a, b) in enumerate(AROUND):

        @pl.when(there(-a, -b))
        def _():
            piece = hrecv.at[n, pl.ds(0, lines(a, b))]
            pltpu.make_async_copy(piece, piece, h_recv.at[n]).wait()

    slot_of = {direction: n for n, direction in enumerate(AROUND)}
    wide[0, :, ch : 2 * ch] = hrecv[slot_of[(1, 0)], 0:cd]
    wide[rd + 1, :, ch : 2 * ch] = hrecv[slot_of[(-1, 0)], 0:cd]
    colf[0] = hrecv[slot_of[(0, 1)], 0:rd].astype(F32)
    colf[1] = hrecv[slot_of[(0, -1)], 0:rd].astype(F32)
    place = lax.broadcasted_iota(jnp.int32, (cd, ch), 0)

    def widen(i, before, after):
        centre = wide[i, :, ch : 2 * ch].astype(F32)
        wide[i, :, 0:ch] = jnp.where(place == 0, before, pltpu.roll(centre, 1, 0)).astype(BF16)
        wide[i, :, 2 * ch : 3 * ch] = jnp.where(
            place == cd - 1, after, pltpu.roll(centre, cd - 1, 0)
        ).astype(BF16)

    def widen_row(i, carry):
        widen(i + 1, colf[0, pl.ds(i, 1), :], colf[1, pl.ds(i, 1), :])
        return carry

    lax.fori_loop(0, rd, widen_row, 0)
    widen(
        0,
        hrecv[slot_of[(1, 1)], 0:16].astype(F32)[0:1],
        hrecv[slot_of[(1, -1)], 0:16].astype(F32)[0:1],
    )
    widen(
        rd + 1,
        hrecv[slot_of[(-1, 1)], 0:16].astype(F32)[0:1],
        hrecv[slot_of[(-1, -1)], 0:16].astype(F32)[0:1],
    )

    strip = 8

    def conv(n, carry):
        total = sym[pl.ds(n * strip, strip)].reshape(strip * cd, ch)
        for a in range(3):
            window = wide[pl.ds(n * strip + a, strip)].reshape(strip * cd, 3 * ch)
            total = total + dot(window, wk_ref[a])
        out_ref[pl.ds(n * strip, strip)] = total.astype(BF16).reshape(strip, cd, ch)
        return carry

    lax.fori_loop(0, rd // strip, conv, 0)

    for k in range(fold):
        to_row, to_col = col * fold + k, row % cn

        @pl.when(jnp.logical_not(jnp.logical_and(to_row == row, to_col == col)))
        def _():
            pltpu.make_async_copy(lsend.at[k], lsend.at[k], l1_send.at[k]).wait()

        to_row, to_col = col * fold + k, row // fold

        @pl.when(jnp.logical_not(jnp.logical_and(to_row == row, to_col == col)))
        def _():
            for step in range(steps):
                src, _dst = to_mirror(step, k)
                pltpu.make_async_copy(src, src, m_send.at[k, step]).wait()

    for d in range(1, rn):
        pltpu.make_async_copy(rg.at[row], rg.at[row], r_send.at[d - 1]).wait()
    for m in range(fold):
        for d in range(1, cn):
            slot = col + m * cn
            pltpu.make_async_copy(lg.at[slot], lg.at[slot], l2_send.at[m, d - 1]).wait()
    for n, (a, b) in enumerate(AROUND):

        @pl.when(there(a, b))
        def _():
            piece = hsend.at[n, pl.ds(0, lines(a, b))]
            pltpu.make_async_copy(piece, piece, h_send.at[n]).wait()


def on_device(
    mesh_shape,
    pair_input,
    alignment_features,
    alignment_mask,
    token_valid,
    left_weight,
    right_weight,
    output_weight,
    gate_weight,
    up_weight,
    down_weight,
    kernel_weight,
):
    rd, cd, ch = pair_input.shape
    sl, tl, aw = alignment_features.shape
    pw = left_weight.shape[1]
    hid = gate_weight.shape[1]
    rn, chans = mesh_shape["row"], mesh_shape["chan"]
    cn = mesh_shape["col"] * chans
    fold = rn // cn
    per = 128 // pw
    cr = min(16, rd)
    depth = rn * sl
    steps = rd // cr
    tall = max(rd, cd, 16)
    feats = jnp.where((alignment_mask != 0)[:, :, None], alignment_features, 0)
    feats = feats.reshape(sl, tl // per, per * aw).transpose(1, 0, 2).reshape(-1, per * aw)
    valid = jnp.broadcast_to(token_valid.astype(F32)[:, None], (token_valid.shape[0], ch))
    wk = kernel_weight.reshape(3, 3 * ch, ch)
    sizes = (rn, cn, chans, fold, rd, cd, ch, sl, tl, pw, cr)
    dma = pltpu.SemaphoreType.DMA
    vmem = pl.BlockSpec(memory_space=pltpu.VMEM)
    return pl.pallas_call(
        functools.partial(block_kernel, sizes),
        out_shape=jax.ShapeDtypeStruct((rd, cd, ch), BF16),
        in_specs=[vmem] * 11,
        out_specs=vmem,
        scratch_shapes=[
            pltpu.VMEM((fold, rd // per + 1, sl, 128), BF16),
            pltpu.VMEM((rn, rd // per + 1, sl, 128), BF16),
            pltpu.VMEM((rn, cd // per + 1, sl, 128), BF16),
            pltpu.VMEM((cd * pw, depth), F32),
            pltpu.VMEM((pw * cd, depth), BF16),
            pltpu.VMEM((steps, depth, cr * pw), BF16),
            pltpu.VMEM((pw * pw, ch), F32),
            pltpu.VMEM((pw * 128, per * ch), BF16),
            pltpu.VMEM((cr // per * cd, pw * 128), BF16),
            pltpu.VMEM((rd, cd, ch), F32),
            pltpu.VMEM((cr, cd, ch), BF16),
            pltpu.VMEM((rd, cd, ch), BF16),
            pltpu.VMEM((cd, rd, ch), BF16),
            pltpu.VMEM((cd * rd, ch), F32),
            pltpu.VMEM((rd, cd, ch), F32),
            pltpu.VMEM((rd + 2, cd, 3 * ch), BF16),
            pltpu.VMEM((2, rd, ch), F32),
            pltpu.VMEM((8, tall, ch), BF16),
            pltpu.VMEM((8, tall, ch), BF16),
            dma((fold,)),
            dma((fold,)),
            dma((fold, cn - 1)),
            dma((fold, cn - 1)),
            dma((rn - 1,)),
            dma((rn - 1,)),
            dma((fold, steps)),
            dma((fold, steps)),
            dma((8,)),
            dma((8,)),
        ],
        compiler_params=pltpu.CompilerParams(
            collective_id=0, has_side_effects=True, vmem_limit_bytes=60 * 1024 * 1024
        ),
    )(
        pair_input,
        feats,
        alignment_mask,
        valid,
        left_weight,
        right_weight,
        output_weight,
        gate_weight,
        up_weight,
        down_weight,
        wk,
    )


def solution(mesh):
    placed = (
        P(("groups", "row"), ("col", "chan"), None),
        P("row", ("groups", "col", "chan"), None),
        P("row", ("groups", "col", "chan")),
        P("groups"),
        P(),
        P(),
        P(),
        P(),
        P(),
        P(),
        P(),
    )
    return jax.shard_map(
        functools.partial(on_device, dict(mesh.shape)),
        mesh=mesh,
        in_specs=placed,
        out_specs=P(("groups", "row"), ("col", "chan"), None),
        check_vma=False,
    )
```

time: 241 us -> 92.8 us (0.39)
  Pallas kernels: 0 us -> 83.1 us
  blocking collectives: 81.4 us -> 0 us
  matrix products: 45.7 us -> 0 us
  starting transfers between devices: 34.4 us -> 0 us
  local copies, waits for them, and re-layouts: 35 us -> 6.2 us
  waiting for transfers between devices: 26.2 us -> 0 us
  loops' own time: 8.13 us -> 0 us
  other arithmetic: 8.75 us -> 2.11 us
    pallas_call x0 -> x1, Pallas kernels: none -> 83.1 us  [on_device(): pl.pallas_call(functools.partial(block_kernel, sizes), out_shape=jax.Shap...]
    all_gather x4 -> x0, blocking collectives: 59.3 us -> none  [the longest x1 28.8 us: on_device(): lax.all_gather(right_local, 'row', axis=0, tiled=True)]
    dot_general x36 -> x0, matrix products: 45.7 us -> none  [the longest x8 21.2 us: transition(): jnp.dot(hidden, down_weight, preferred_element_type=jnp.float32)]
    all_to_all x1 -> x0, blocking collectives: 22.1 us -> none  [on_device(): lax.all_to_all(pair_one, ('col', 'chan'), split_axis=0, concat_axis=1, ti...]
    all_to_all x4 -> x0, waiting for transfers between devices: 21.1 us -> none  [the longest x1 21.1 us: on_device(): lax.all_to_all(lax.all_to_all(pair_one, ('col', 'chan'), split_axis=0, co...]
    all_to_all x4 -> x0, starting transfers between devices: 20.3 us -> none  [the longest x1 6.49 us: on_device(): lax.all_to_all(flipped, ('col', 'chan'), split_axis=1, concat_axis=1, til...]
    ppermute x4 -> x0, starting transfers between devices: 14.1 us -> none  [the longest x2 7.06 us: with_halo(): after = lax.ppermute(initial, axis, down)]
    all_to_all x8 -> x0, local copies, waits for them, and re-layouts: 9.62 us -> none  [the longest x2 4.64 us: on_device(): lax.all_to_all(wide_left, 'row', split_axis=1, concat_axis=0, tiled=True)]
  transfers between devices with their start and end apart: 8 -> 0, of which waited for: 3 -> 0; matrix products, arithmetic and copies ran while one was open for 10% -> 0% of each run, Pallas kernels for 0% -> 0%
where the time goes in v1:
time: 92.8 us; the launch traced here: 91.5 us
  Pallas kernels  83.1 us (90%)
  local copies, waits for them, and re-layouts  6.2 us (7%)
  other arithmetic  2.11 us (2%)
    pallas_call x1, Pallas kernels, on_device(): pl.pallas_call(functools.partial(block_kernel, sizes), out_shape=jax.Shap...  83.1 us
    unnamed x9, local copies, waits for them, and re-layouts  4.34 us

profile of v1, /device:TPU:9, one launch (start us, length us, event | category | flops | bytes accessed | tf_op | source)
XLA Modules:
  0.0 91.5 jit_solution(1674634221591174821)
XLA Ops:
  0.0 0.0 copy-start.2
  0.0 0.7 copy-done.2
  0.7 0.0 copy-start
  0.7 0.7 broadcast_compare_fusion
  1.4 0.0 copy-done
  1.4 0.0 copy-start.1
  1.4 0.7 copy.13.wl_ref
  2.1 0.0 copy-done.1
  2.1 0.7 copy.14.wr_ref
  2.8 0.7 broadcast_in_dim.21.valid_ref
  3.6 1.4 %broadcast_select_fusion = bf16[32,64,64]{2,1,0:T(8,128)(2,1)S(1)} fusion(bf16[32,64,64]{2,1,0:T(8,128)(2,1)} %param.12, pred[32,64]{1,0:T(8,128)(4,1)S(1)} %broadcast_compare_fusion), kind=kLoop, calls=%fused_computation | loop fusion | flops 131072 | bytes 526336 | tf_op jit(solution)/shard_map/jit(_where)/select_n | solution.py:383
  5.0 0.3 reshape.11
  5.3 0.8 copy.12
  6.1 83.1 %shard_map.109 = bf16[64,64,128]{2,1,0:T(8,128)(2,1)} custom-call(bf16[64,64,128]{2,1,0:T(8,128)(2,1)} %pair_ref.1, bf16[512,256]{1,0:T(8,128)(2,1)} %bitcast.4, s32[32,64]{1,0:T(8,128)} %mask_ref.1, f32[256,128]{1,0:T(8,128)} %broadcast_in_dim.21.valid_ref, bf16[64,32]{1,0:T(8,128)(2,1)} %copy.13.wl_ref, bf16[64,32]{1,0:T(8,128)(2,1)} %copy.14.wr_ref, ...), custom_call_target="tpu_custom_call" | custom-call | tf_op jit(solution)/shard_map/pallas_call | solution.py:390
  89.2 2.3 %copy.16 = bf16[64,64,128]{2,1,0:T(8,128)(2,1)} copy(bf16[64,64,128]{2,1,0:T(8,128)(2,1)} %shard_map.109) | data formatting | bytes 2097152
  (1 shorter events, 0.0 us)
Async XLA Ops:
  0.0 0.7 copy-start.2
  0.7 0.7 copy-start
  1.4 0.7 copy-start.1

commit v2 on v1

--- a/solution.py
+++ b/solution.py
@@ -58,6 +58,9 @@
     r_recv,
     m_send,
     m_recv,
+    relay,
+    rl_send,
+    rl_recv,
     h_send,
     h_recv,
 ):
@@ -176,10 +179,66 @@
 
     qstep = min(8, pw)
 
-    def to_mirror(step, k):
-        src = two.at[pl.ds(step * cr, cr), pl.ds(k * rd, rd)]
-        dst = mirror.at[pl.ds((row % fold) * rd + step * cr, cr)]
+    part = cr // 2
+
+    def to_mirror(step, k, p):
+        begin = step * cr + p * part
+        src = two.at[pl.ds(begin, part), pl.ds(k * rd, rd)]
+        dst = mirror.at[pl.ds((row % fold) * rd + begin, part)]
         return src, dst
+
+    def send_mirror(step, k):
+        to_row, to_col = col * fold + k, row // fold
+        mine = jnp.logical_and(to_row == row, to_col == col)
+        across = to_col // chans != col // chans
+        for p in (1, 0):
+            src, dst = to_mirror(step, k, p)
+            rsem = m_recv.at[row % fold, step, p]
+            ssem = m_send.at[k, step, p]
+
+            @pl.when(mine)
+            def _():
+                pltpu.make_async_copy(src, dst, rsem).start()
+
+            direct = jnp.logical_not(mine)
+            if p == 1:
+                direct = jnp.logical_and(direct, jnp.logical_not(across))
+
+                @pl.when(across)
+                def _():
+                    slot, core = to_row // chans, to_row % chans
+                    remote(
+                        src, relay.at[slot, step], ssem, rl_recv.at[slot, step], row,
+                        to_col // chans * chans + core,
+                    ).start()
+
+            @pl.when(direct)
+            def _():
+                remote(src, dst, ssem, rsem, to_row, to_col).start()
+
+    def relayed(m):
+        key = m * chans + col % chans
+        from_col, to_row, to_col = key // fold, key, row // fold
+        active = jnp.logical_and(
+            to_col // chans == col // chans, from_col // chans != to_col // chans
+        )
+        return active, row, to_row, to_col
+
+    def forward(step):
+        for m in range(rn // chans):
+            active, from_row, to_row, to_col = relayed(m)
+
+            @pl.when(active)
+            def _():
+                piece = relay.at[m, step]
+                pltpu.make_async_copy(piece, piece, rl_recv.at[m, step]).wait()
+                begin = (from_row % fold) * rd + step * cr + part
+                remote(
+                    piece, mirror.at[pl.ds(begin, part)], rl_send.at[m, step],
+                    m_recv.at[from_row % fold, step, 1], to_row, to_col,
+                ).start()
+
+    lag = min(1, steps)
 
     def one_step(step, carry):
         lpart = lcat[step]
@@ -209,27 +268,23 @@
             result = (values + dot(hidden, wd_ref[...])).astype(BF16)
             two[pl.ds(step * cr + h, half)] = result.reshape(half, cd, ch)
         for k in range(fold):
-            to_row, to_col = col * fold + k, row // fold
-            mine = jnp.logical_and(to_row == row, to_col == col)
-            src, dst = to_mirror(step, k)
-            rsem = m_recv.at[row % fold, step]
-
-            @pl.when(mine)
-            def _():
-                pltpu.make_async_copy(src, dst, rsem).start()
-
-            @pl.when(jnp.logical_not(mine))
-            def _():
-                remote(src, dst, m_send.at[k, step], rsem, to_row, to_col).start()
+            send_mirror(step, k)
+
+        @pl.when(step >= lag)
+        def _():
+            forward(step - lag)
 
         return carry
 
     lax.fori_loop(0, steps, one_step, 0)
+    for step in range(steps - lag, steps):
+        forward(step)
 
     for step in range(steps):
         for k in range(fold):
-            piece = mirror.at[pl.ds(k * rd + step * cr, cr)]
-            pltpu.make_async_copy(piece, piece, m_recv.at[k, step]).wait()
+            for p in (0, 1):
+                piece = mirror.at[pl.ds(k * rd + step * cr + p * part, part)]
+                pltpu.make_async_copy(piece, piece, m_recv.at[k, step, p]).wait()
             begin = k * rd + step * cr
             mf[begin * rd : (begin + cr) * rd, :] = (
                 mirror[begin : begin + cr].astype(F32).reshape(cr * rd, ch)
@@ -337,8 +392,17 @@
         @pl.when(jnp.logical_not(jnp.logical_and(to_row == row, to_col == col)))
         def _():
             for step in range(steps):
-                src, _dst = to_mirror(step, k)
-                pltpu.make_async_copy(src, src, m_send.at[k, step]).wait()
+                for p in (0, 1):
+                    src, _dst = to_mirror(step, k, p)
+                    pltpu.make_async_copy(src, src, m_send.at[k, step, p]).wait()
+
+    for m in range(rn // chans):
+
+        @pl.when(relayed(m)[0])
+        def _():
+            for step in range(steps):
+                piece = relay.at[m, step]
+                pltpu.make_async_copy(piece, piece, rl_send.at[m, step]).wait()
 
     for d in range(1, rn):
         pltpu.make_async_copy(rg.at[row], rg.at[row], r_send.at[d - 1]).wait()
@@ -418,8 +482,11 @@
             dma((fold, cn - 1)),
             dma((rn - 1,)),
             dma((rn - 1,)),
-            dma((fold, steps)),
-            dma((fold, steps)),
+            dma((fold, steps, 2)),
+            dma((fold, steps, 2)),
+            pltpu.VMEM((rn // chans, steps, cr // 2, rd, ch), BF16),
+            dma((rn // chans, steps)),
+            dma((rn // chans, steps)),
             dma((8,)),
             dma((8,)),
         ],

time: 92.8 us -> 78.4 us (0.84)
  Pallas kernels: 83.1 us -> 69.7 us
    pallas_call x1, Pallas kernels: 83.1 us -> 69.7 us  [on_device(): pl.pallas_call(functools.partial(block_kernel, sizes), out_shape=jax.Shap...]
where the time goes in v2:
time: 78.4 us; the launch traced here: 78 us
  Pallas kernels  69.7 us (89%)
  local copies, waits for them, and re-layouts  6.2 us (8%)
  other arithmetic  2.11 us (3%)
    pallas_call x1, Pallas kernels, on_device(): pl.pallas_call(functools.partial(block_kernel, sizes), out_shape=jax.Shap...  69.7 us
    unnamed x9, local copies, waits for them, and re-layouts  4.34 us

profile of v2, /device:TPU:9, one launch (start us, length us, event | category | flops | bytes accessed | tf_op | source)
XLA Modules:
  0.0 78.0 jit_solution(3345737362522940661)
XLA Ops:
  0.0 0.0 copy-start.2
  0.0 0.7 copy-done.2
  0.7 0.0 copy-start
  0.7 0.7 broadcast_compare_fusion
  1.4 0.0 copy-done
  1.4 0.0 copy-start.1
  1.4 0.7 copy.13.wl_ref
  2.1 0.0 copy-done.1
  2.1 0.7 copy.14.wr_ref
  2.8 0.7 broadcast_in_dim.21.valid_ref
  3.6 1.4 %broadcast_select_fusion = bf16[32,64,64]{2,1,0:T(8,128)(2,1)S(1)} fusion(bf16[32,64,64]{2,1,0:T(8,128)(2,1)} %param.12, pred[32,64]{1,0:T(8,128)(4,1)S(1)} %broadcast_compare_fusion), kind=kLoop, calls=%fused_computation | loop fusion | flops 131072 | bytes 526336 | tf_op jit(solution)/shard_map/jit(_where)/select_n | solution.py:447
  5.0 0.3 reshape.11
  5.3 0.8 %copy.12 = bf16[32,16,256]{2,0,1:T(8,128)(2,1)} copy(bf16[32,16,256]{2,1,0:T(8,128)(2,1)S(1)} %reshape.11) | data formatting | bytes 524288 | tf_op jit(solution)/shard_map/reshape | solution.py:448
  6.1 69.7 %shard_map.109 = bf16[64,64,128]{2,1,0:T(8,128)(2,1)} custom-call(bf16[64,64,128]{2,1,0:T(8,128)(2,1)} %pair_ref.1, bf16[512,256]{1,0:T(8,128)(2,1)} %bitcast.4, s32[32,64]{1,0:T(8,128)} %mask_ref.1, f32[256,128]{1,0:T(8,128)} %broadcast_in_dim.21.valid_ref, bf16[64,32]{1,0:T(8,128)(2,1)} %copy.13.wl_ref, bf16[64,32]{1,0:T(8,128)(2,1)} %copy.14.wr_ref, ...), custom_call_target="tpu_custom_call" | custom-call | tf_op jit(solution)/shard_map/pallas_call | solution.py:454
  75.7 2.3 %copy.16 = bf16[64,64,128]{2,1,0:T(8,128)(2,1)} copy(bf16[64,64,128]{2,1,0:T(8,128)(2,1)} %shard_map.109) | data formatting | bytes 2097152
  (1 shorter events, 0.0 us)
Async XLA Ops:
  0.0 0.7 copy-start.2
  0.7 0.7 copy-start
  1.4 0.7 copy-start.1

commit v3 on v2

--- a/solution.py
+++ b/solution.py
@@ -19,18 +19,19 @@
 
 def block_kernel(
     sizes,
-    pair_ref,
     feat_ref,
     mask_ref,
     valid_ref,
     wl_ref,
     wr_ref,
-    wo_ref,
-    wg_ref,
-    wu_ref,
-    wd_ref,
-    wk_ref,
-    out_ref,
+    *rest,
+):
+    far, (out_ref, *rest) = rest[:6], rest[6:]
+    near, (w_sem, *rest) = rest[:6], rest[6:]
+    pair_ref, wo_ref, wg_ref, wu_ref, wd_ref, wk_ref = near
+    (
+    proj,
+    vrows,
     lsend,
     lg,
     rg,
@@ -63,7 +64,7 @@
     rl_recv,
     h_send,
     h_recv,
-):
+    ) = rest
     rn, cn, chans, fold, rd, cd, ch, sl, tl, pw, cr = sizes
     row = lax.axis_index("row")
     col = lax.axis_index("col") * chans + lax.axis_index("chan")
@@ -82,6 +83,10 @@
             device_id=at(r, c), device_id_type=MESH,
         )
 
+    order = (1, 0, 2, 3, 4, 5)
+    loads = [pltpu.make_async_copy(far[n], near[n], w_sem.at[n]) for n in range(6)]
+    for n in order:
+        loads[n].start()
     hrecv[...] = jnp.zeros_like(hrecv)
     barrier = pltpu.get_barrier_semaphore()
 
@@ -91,29 +96,43 @@
 
     lax.fori_loop(0, rn * cn, greet, 0)
 
-    aw = wl_ref.shape[0]
     spread = (
         lax.broadcasted_iota(jnp.int32, (pw, 128), 1) % pw
         == lax.broadcasted_iota(jnp.int32, (pw, 128), 0)
     ).astype(F32).astype(BF16)
-    own = (
-        lax.broadcasted_iota(jnp.int32, (per * aw, 128), 0) // aw
-        == lax.broadcasted_iota(jnp.int32, (per * aw, 128), 1) // pw
-    )
-
-    def block_weight(w):
-        tiled = dot(w, spread)
-        return jnp.where(own, jnp.concatenate([tiled] * per, axis=0), 0.0).astype(BF16)
-
-    feats = feat_ref[...]
-    left = dot(feats, block_weight(wl_ref[...])).reshape(tl // per, sl, 128).astype(BF16)
-    right = dot(feats, block_weight(wr_ref[...])).reshape(tl // per, sl, 128).astype(BF16)
     mask = mask_ref[...].astype(F32).astype(BF16)
+    spots = tl // per
+    token_of = (
+        lax.broadcasted_iota(jnp.int32, (tl, spots * 128), 1) // pw
+        == lax.broadcasted_iota(jnp.int32, (tl, spots * 128), 0)
+    ).astype(F32).astype(BF16)
+    wide_mask = dot(mask, token_of)
+    feats = feat_ref[...].reshape(sl * tl, feat_ref.shape[2])
+    lane_of = lax.broadcasted_iota(jnp.int32, (sl, 128), 1) // pw
+
+    def project(n, w_ref):
+        tiled = lax.dot_general(
+            w_ref[...], spread, (((0,), (0,)), ((), ())), preferred_element_type=F32
+        ).astype(BF16)
+        proj[n] = dot(feats, tiled)
+        parts = []
+        for g in range(spots):
+            got = proj[n, pl.ds(g * per, sl, stride=tl), :]
+            for t in range(1, per):
+                other = proj[n, pl.ds(g * per + t, sl, stride=tl), :]
+                got = jnp.where(lane_of == t, other, got)
+            parts.append((got * wide_mask[:, g * 128 : (g + 1) * 128]).astype(BF16))
+        return parts
+
+    left = project(0, wl_ref)
+    right = project(1, wr_ref)
     for k in range(fold):
-        lsend[k, 0:lgroups] = left[k * lgroups : (k + 1) * lgroups]
+        for g in range(lgroups):
+            lsend[k, g] = left[k * lgroups + g]
         lsend[k, lgroups] = jnp.zeros((sl, 128), BF16)
         lsend[k, lgroups, :, 0:rd] = mask[:, k * rd : (k + 1) * rd]
-    rg[row, 0:rgroups] = right
+    for g in range(rgroups):
+        rg[row, g] = right[g]
     rg[row, rgroups] = jnp.zeros((sl, 128), BF16)
     rg[row, rgroups, :, 0:tl] = mask
 
@@ -132,11 +151,37 @@
         def _():
             remote(lsend.at[k], lg.at[row], l1_send.at[k], l1_recv.at[slot], to_row, to_col).start()
 
-    for d in range(1, rn):
-        remote(
-            rg.at[row], rg.at[row], r_send.at[d - 1], r_recv.at[d - 1], (row + d) % rn, col
-        ).start()
-
+    def chain(t):
+        low, high = jnp.maximum(row - t, 0), jnp.minimum(row + t, rn - 1)
+        ups = jnp.logical_and(row - t >= 0, row + 1 < rn)
+        downs = jnp.logical_and(row + t < rn, row >= 1)
+        return (ups, low, row + 1), (downs, high, row - 1)
+
+    def pass_on(t):
+        for way, (go, slot, to_row) in enumerate(chain(t)):
+
+            @pl.when(go)
+            def _():
+                remote(
+                    rg.at[slot], rg.at[slot], r_send.at[way, t], r_recv.at[slot], to_row, col
+                ).start()
+
+    pass_on(0)
+
+    tokens = valid_ref.shape[1]
+    valid = valid_ref[...].astype(F32)
+
+    def as_rows(first, count):
+        hit = lax.broadcasted_iota(jnp.int32, (count, tokens), 1) == first + (
+            lax.broadcasted_iota(jnp.int32, (count, tokens), 0)
+        )
+        chosen = jnp.where(hit, jnp.broadcast_to(valid, (count, tokens)), 0.0).astype(BF16)
+        return dot(chosen, jnp.ones((tokens, ch), BF16))
+
+    vrows[0:rd] = as_rows(row * rd, rd)
+    valid_cols = as_rows(col * cd, cd)
+
+    loads[1].wait()
     wof[...] = wo_ref[...].astype(F32)
     w4[...] = jnp.zeros_like(w4)
     for q in range(pw):
@@ -153,9 +198,18 @@
                 row, (col + d) % cn,
             ).start()
 
-    for d in range(1, rn):
-        slot = (row + rn - d) % rn
-        pltpu.make_async_copy(rg.at[slot], rg.at[slot], r_recv.at[d - 1]).wait()
+    for t in range(rn - 1):
+        if t:
+            pass_on(t)
+        for there_is, slot in (
+            (row - t - 1 >= 0, jnp.maximum(row - t - 1, 0)),
+            (row + t + 1 < rn, jnp.minimum(row + t + 1, rn - 1)),
+        ):
+
+            @pl.when(there_is)
+            def _():
+                pltpu.make_async_copy(rg.at[slot], rg.at[slot], r_recv.at[slot]).wait()
+
     for g in range(rgroups):
         slab = rg[:, g].astype(F32).reshape(depth, 128)
         rt[g * 128 : (g + 1) * 128, :] = slab.T
@@ -176,6 +230,9 @@
     inverse = 1.0 / jnp.maximum(counts, 1.0)
     for i in range(rd):
         rexp[i] = jnp.broadcast_to(inverse[0:cd, i : i + 1], (cd, ch))
+
+    for n in (0, 2, 3, 4, 5):
+        loads[n].wait()
 
     qstep = min(8, pw)
 
@@ -282,26 +339,28 @@
 
     for step in range(steps):
         for k in range(fold):
+            begin = k * rd + step * cr
             for p in (0, 1):
-                piece = mirror.at[pl.ds(k * rd + step * cr + p * part, part)]
+                piece = mirror.at[pl.ds(begin + p * part, part)]
                 pltpu.make_async_copy(piece, piece, m_recv.at[k, step, p]).wait()
-            begin = k * rd + step * cr
             mf[begin * rd : (begin + cr) * rd, :] = (
                 mirror[begin : begin + cr].astype(F32).reshape(cr * rd, ch)
             )
-
-    valid_cols = valid_ref[pl.ds(pl.multiple_of(col * cd, 8), cd), :]
-
-    def one_row(i, carry):
-        half_sum = (two[i].astype(F32) + mf[pl.ds(i, cd, stride=rd), :]) * 0.5
-        sym[i] = half_sum
-        masked = half_sum * valid_cols * valid_ref[pl.ds(row * rd + i, 1), :]
-        wide[i + 1, :, ch : 2 * ch] = masked.astype(BF16)
-        colf[0, pl.ds(i, 1), :] = masked[0:1]
-        colf[1, pl.ds(i, 1), :] = masked[cd - 1 : cd]
-        return carry
-
-    lax.fori_loop(0, rd, one_row, 0)
+            some_cols = valid_cols[begin : begin + cr]
+
+            def one_row(i, carry):
+                other = mf[pl.ds(begin * rd + i, cr, stride=rd), :]
+                half_sum = (two[i, begin : begin + cr].astype(F32) + other) * 0.5
+                sym[i, begin : begin + cr] = half_sum
+                masked = half_sum * some_cols * vrows[pl.ds(i, 1), :]
+                wide[i + 1, begin : begin + cr, ch : 2 * ch] = masked.astype(BF16)
+                if begin == 0:
+                    colf[0, pl.ds(i, 1), :] = masked[0:1]
+                if begin + cr == cd:
+                    colf[1, pl.ds(i, 1), :] = masked[cr - 1 : cr]
+                return carry
+
+            lax.fori_loop(0, rd, one_row, 0, unroll=4)
 
     for n, (a, b) in enumerate(AROUND):
         if b == 0:
@@ -331,18 +390,6 @@
                 h_recv.at[n], row + a, col + b,
             ).start()
 
-    for n, (a, b) in enumerate(AROUND):
-
-        @pl.when(there(-a, -b))
-        def _():
-            piece = hrecv.at[n, pl.ds(0, lines(a, b))]
-            pltpu.make_async_copy(piece, piece, h_recv.at[n]).wait()
-
-    slot_of = {direction: n for n, direction in enumerate(AROUND)}
-    wide[0, :, ch : 2 * ch] = hrecv[slot_of[(1, 0)], 0:cd]
-    wide[rd + 1, :, ch : 2 * ch] = hrecv[slot_of[(-1, 0)], 0:cd]
-    colf[0] = hrecv[slot_of[(0, 1)], 0:rd].astype(F32)
-    colf[1] = hrecv[slot_of[(0, -1)], 0:rd].astype(F32)
     place = lax.broadcasted_iota(jnp.int32, (cd, ch), 0)
 
     def widen(i, before, after):
@@ -353,10 +400,37 @@
         ).astype(BF16)
 
     def widen_row(i, carry):
-        widen(i + 1, colf[0, pl.ds(i, 1), :], colf[1, pl.ds(i, 1), :])
+        widen(i + 1, 0.0, 0.0)
         return carry
 
-    lax.fori_loop(0, rd, widen_row, 0)
+    lax.fori_loop(0, rd, widen_row, 0, unroll=4)
+
+    for n, (a, b) in enumerate(AROUND):
+
+        @pl.when(there(-a, -b))
+        def _():
+            piece = hrecv.at[n, pl.ds(0, lines(a, b))]
+            pltpu.make_async_copy(piece, piece, h_recv.at[n]).wait()
+
+    slot_of = {direction: n for n, direction in enumerate(AROUND)}
+    wide[0, :, ch : 2 * ch] = hrecv[slot_of[(1, 0)], 0:cd]
+    wide[rd + 1, :, ch : 2 * ch] = hrecv[slot_of[(-1, 0)], 0:cd]
+    colf[0] = hrecv[slot_of[(0, 1)], 0:rd].astype(F32)
+    colf[1] = hrecv[slot_of[(0, -1)], 0:rd].astype(F32)
+    edge = lax.broadcasted_iota(jnp.int32, (16, ch), 0)
+
+    def patch_row(i, carry):
+        first = wide[i + 1, 0:16, 0:ch].astype(F32)
+        wide[i + 1, 0:16, 0:ch] = jnp.where(
+            edge == 0, colf[0, pl.ds(i, 1), :], first
+        ).astype(BF16)
+        last = wide[i + 1, cd - 16 : cd, 2 * ch : 3 * ch].astype(F32)
+        wide[i + 1, cd - 16 : cd, 2 * ch : 3 * ch] = jnp.where(
+            edge == 15, colf[1, pl.ds(i, 1), :], last
+        ).astype(BF16)
+        return carry
+
+    lax.fori_loop(0, rd, patch_row, 0, unroll=4)
     widen(
         0,
         hrecv[slot_of[(1, 1)], 0:16].astype(F32)[0:1],
@@ -404,8 +478,13 @@
                 piece = relay.at[m, step]
                 pltpu.make_async_copy(piece, piece, rl_send.at[m, step]).wait()
 
-    for d in range(1, rn):
-        pltpu.make_async_copy(rg.at[row], rg.at[row], r_send.at[d - 1]).wait()
+    for t in range(rn - 1):
+        for way, (go, slot, _to_row) in enumerate(chain(t)):
+
+            @pl.when(go)
+            def _():
+                pltpu.make_async_copy(rg.at[slot], rg.at[slot], r_send.at[way, t]).wait()
+
     for m in range(fold):
         for d in range(1, cn):
             slot = col + m * cn
@@ -444,19 +523,21 @@
     depth = rn * sl
     steps = rd // cr
     tall = max(rd, cd, 16)
-    feats = jnp.where((alignment_mask != 0)[:, :, None], alignment_features, 0)
-    feats = feats.reshape(sl, tl // per, per * aw).transpose(1, 0, 2).reshape(-1, per * aw)
-    valid = jnp.broadcast_to(token_valid.astype(F32)[:, None], (token_valid.shape[0], ch))
     wk = kernel_weight.reshape(3, 3 * ch, ch)
     sizes = (rn, cn, chans, fold, rd, cd, ch, sl, tl, pw, cr)
+    large = (pair_input, output_weight, gate_weight, up_weight, down_weight, wk)
     dma = pltpu.SemaphoreType.DMA
     vmem = pl.BlockSpec(memory_space=pltpu.VMEM)
     return pl.pallas_call(
         functools.partial(block_kernel, sizes),
         out_shape=jax.ShapeDtypeStruct((rd, cd, ch), BF16),
-        in_specs=[vmem] * 11,
+        in_specs=[vmem] * 5 + [pl.BlockSpec(memory_space=pl.ANY)] * 6,
         out_specs=vmem,
         scratch_shapes=[
+            *[pltpu.VMEM(value.shape, value.dtype) for value in large],
+            dma((6,)),
+            pltpu.VMEM((2, sl * tl, 128), F32),
+            pltpu.VMEM((tall, ch), F32),
             pltpu.VMEM((fold, rd // per + 1, sl, 128), BF16),
             pltpu.VMEM((rn, rd // per + 1, sl, 128), BF16),
             pltpu.VMEM((rn, cd // per + 1, sl, 128), BF16),
@@ -480,8 +561,8 @@
             dma((fold,)),
             dma((fold, cn - 1)),
             dma((fold, cn - 1)),
-            dma((rn - 1,)),
-            dma((rn - 1,)),
+            dma((2, rn - 1)),
+            dma((rn,)),
             dma((fold, steps, 2)),
             dma((fold, steps, 2)),
             pltpu.VMEM((rn // chans, steps, cr // 2, rd, ch), BF16),
@@ -494,17 +575,12 @@
             collective_id=0, has_side_effects=True, vmem_limit_bytes=60 * 1024 * 1024
         ),
     )(
-        pair_input,
-        feats,
+        alignment_features,
         alignment_mask,
-        valid,
-        left_weight,
-        right_weight,
-        output_weight,
-        gate_weight,
-        up_weight,
-        down_weight,
-        wk,
+        token_valid.reshape(1, -1),
+        left_weight.T,
+        right_weight.T,
+        *large,
     )
 
 

time: 78.4 us -> 64.8 us (0.83)
  Pallas kernels: 69.7 us -> 62.3 us
  local copies, waits for them, and re-layouts: 6.2 us -> 2.26 us
  other arithmetic: 2.11 us -> 0 us
    pallas_call x1, Pallas kernels: 69.7 us -> 62.3 us  [on_device(): pl.pallas_call(functools.partial(block_kernel, sizes), out_shape=jax.Shap...]
    unnamed x9 -> x1, local copies, waits for them, and re-layouts: 4.34 us -> 2.26 us
    select_n x1 -> x0, other arithmetic: 1.38 us -> none  [on_device(): feats = jnp.where((alignment_mask != 0)[:, :, None], alignment_features, 0)]
    reshape x2 -> x0, local copies, waits for them, and re-layouts: 1.12 us -> none  [on_device(): feats.reshape(sl, tl // per, per * aw).transpose(1, 0, 2)]
where the time goes in v3:
time: 64.8 us; the launch traced here: 64.6 us
  Pallas kernels  62.3 us (96%)
  local copies, waits for them, and re-layouts  2.26 us (3%)
    pallas_call x1, Pallas kernels, on_device(): pl.pallas_call(functools.partial(block_kernel, sizes), out_shape=jax.Shap...  62.3 us
    unnamed x1, local copies, waits for them, and re-layouts  2.26 us

profile of v3, /device:TPU:9, one launch (start us, length us, event | category | flops | bytes accessed | tf_op | source)
XLA Modules:
  0.0 64.6 jit_solution(3488843153020849250)
XLA Ops:
  0.0 62.3 %shard_map.109 = bf16[64,64,128]{2,1,0:T(8,128)(2,1)} custom-call(bf16[32,64,64]{2,1,0:T(8,128)(2,1)} %feat_ref.1, s32[32,64]{1,0:T(8,128)} %mask_ref.1, s32[1,256]{1,0:T(1,128)} %bitcast.7, bf16[32,64]{1,0:T(8,128)(2,1)} %bitcast.5, bf16[32,64]{1,0:T(8,128)(2,1)} %bitcast.6, bf16[64,64,128]{2,1,0:T(8,128)(2,1)} %rest_0_.1, bf16[1024,128]{1,0:T(8,128)(2,1)} %rest_1_.1, ...), custom_call_target="tpu_custom_call" | custom-call | tf_op jit(solution)/shard_map/pallas_call | solution.py:531
  62.3 2.3 %copy.13 = bf16[64,64,128]{2,1,0:T(8,128)(2,1)} copy(bf16[64,64,128]{2,1,0:T(8,128)(2,1)} %shard_map.109) | data formatting | bytes 2097152

commit v4 on v3

--- a/solution.py
+++ b/solution.py
@@ -157,14 +157,19 @@
         downs = jnp.logical_and(row + t < rn, row >= 1)
         return (ups, low, row + 1), (downs, high, row - 1)
 
+    cut = rgroups // 2
+    pieces = (pl.ds(0, cut), pl.ds(cut, rgroups + 1 - cut))
+
     def pass_on(t):
         for way, (go, slot, to_row) in enumerate(chain(t)):
 
             @pl.when(go)
             def _():
-                remote(
-                    rg.at[slot], rg.at[slot], r_send.at[way, t], r_recv.at[slot], to_row, col
-                ).start()
+                for e, piece in enumerate(pieces):
+                    part_of = rg.at[slot, piece]
+                    remote(
+                        part_of, part_of, r_send.at[way, t, e], r_recv.at[slot, e], to_row, col
+                    ).start()
 
     pass_on(0)
 
@@ -199,16 +204,27 @@
             ).start()
 
     for t in range(rn - 1):
-        if t:
-            pass_on(t)
-        for there_is, slot in (
-            (row - t - 1 >= 0, jnp.maximum(row - t - 1, 0)),
-            (row + t + 1 < rn, jnp.minimum(row + t + 1, rn - 1)),
-        ):
-
-            @pl.when(there_is)
-            def _():
-                pltpu.make_async_copy(rg.at[slot], rg.at[slot], r_recv.at[slot]).wait()
+        for e, piece in enumerate(pieces):
+            for way, (there_is, slot) in enumerate((
+                (row - t - 1 >= 0, jnp.maximum(row - t - 1, 0)),
+                (row + t + 1 < rn, jnp.minimum(row + t + 1, rn - 1)),
+            )):
+
+                @pl.when(there_is)
+                def _():
+                    part_of = rg.at[slot, piece]
+                    pltpu.make_async_copy(part_of, part_of, r_recv.at[slot, e]).wait()
+
+                if t + 1 < rn - 1:
+                    go, _slot, to_row = chain(t + 1)[way]
+
+                    @pl.when(go)
+                    def _():
+                        part_of = rg.at[slot, piece]
+                        remote(
+                            part_of, part_of, r_send.at[way, t + 1, e], r_recv.at[slot, e],
+                            to_row, col,
+                        ).start()
 
     for g in range(rgroups):
         slab = rg[:, g].astype(F32).reshape(depth, 128)
@@ -244,34 +260,33 @@
         dst = mirror.at[pl.ds((row % fold) * rd + begin, part)]
         return src, dst
 
-    def send_mirror(step, k):
+    def send_mirror(step, k, p):
         to_row, to_col = col * fold + k, row // fold
         mine = jnp.logical_and(to_row == row, to_col == col)
         across = to_col // chans != col // chans
-        for p in (1, 0):
-            src, dst = to_mirror(step, k, p)
-            rsem = m_recv.at[row % fold, step, p]
-            ssem = m_send.at[k, step, p]
-
-            @pl.when(mine)
+        src, dst = to_mirror(step, k, p)
+        rsem = m_recv.at[row % fold, step, p]
+        ssem = m_send.at[k, step, p]
+
+        @pl.when(mine)
+        def _():
+            pltpu.make_async_copy(src, dst, rsem).start()
+
+        direct = jnp.logical_not(mine)
+        if p == 1:
+            direct = jnp.logical_and(direct, jnp.logical_not(across))
+
+            @pl.when(across)
             def _():
-                pltpu.make_async_copy(src, dst, rsem).start()
-
-            direct = jnp.logical_not(mine)
-            if p == 1:
-                direct = jnp.logical_and(direct, jnp.logical_not(across))
-
-                @pl.when(across)
-                def _():
-                    slot, core = to_row // chans, to_row % chans
-                    remote(
-                        src, relay.at[slot, step], ssem, rl_recv.at[slot, step], row,
-                        to_col // chans * chans + core,
-                    ).start()
-
-            @pl.when(direct)
-            def _():
-                remote(src, dst, ssem, rsem, to_row, to_col).start()
+                slot, core = to_row // chans, to_row % chans
+                remote(
+                    src, relay.at[slot, step], ssem, rl_recv.at[slot, step], row,
+                    to_col // chans * chans + core,
+                ).start()
+
+        @pl.when(direct)
+        def _():
+            remote(src, dst, ssem, rsem, to_row, to_col).start()
 
     def relayed(m):
         key = m * chans + col % chans
@@ -312,9 +327,8 @@
                 at_row = step * cr + g * per + i
                 add = update[g * cd : (g + 1) * cd, i * ch : (i + 1) * ch] * rexp[at_row]
                 ones[g * per + i] = (pair_ref[at_row].astype(F32) + add).astype(BF16)
-        half = max(1, cr // 2)
-        for h in range(0, cr, half):
-            values = ones[h : h + half].reshape(half * cd, ch).astype(F32)
+        for p in (1, 0):
+            values = ones[p * part : (p + 1) * part].reshape(part * cd, ch).astype(F32)
             centre = jnp.mean(values, axis=-1, keepdims=True)
             shifted = values - centre
             var = jnp.mean(jnp.square(shifted), axis=-1, keepdims=True)
@@ -323,13 +337,14 @@
             up = dot(normed, wu_ref[...])
             hidden = (gate / (1.0 + jnp.exp(-gate)) * up).astype(BF16)
             result = (values + dot(hidden, wd_ref[...])).astype(BF16)
-            two[pl.ds(step * cr + h, half)] = result.reshape(half, cd, ch)
-        for k in range(fold):
-            send_mirror(step, k)
-
-        @pl.when(step >= lag)
-        def _():
-            forward(step - lag)
+            two[pl.ds(step * cr + p * part, part)] = result.reshape(part, cd, ch)
+            for k in range(fold):
+                send_mirror(step, k, p)
+            if p == 1:
+
+                @pl.when(step >= lag)
+                def _():
+                    forward(step - lag)
 
         return carry
 
@@ -483,7 +498,9 @@
 
             @pl.when(go)
             def _():
-                pltpu.make_async_copy(rg.at[slot], rg.at[slot], r_send.at[way, t]).wait()
+                for e, piece in enumerate(pieces):
+                    part_of = rg.at[slot, piece]
+                    pltpu.make_async_copy(part_of, part_of, r_send.at[way, t, e]).wait()
 
     for m in range(fold):
         for d in range(1, cn):
@@ -561,8 +578,8 @@
             dma((fold,)),
             dma((fold, cn - 1)),
             dma((fold, cn - 1)),
-            dma((2, rn - 1)),
-            dma((rn,)),
+            dma((2, rn - 1, 2)),
+            dma((rn, 2)),
             dma((fold, steps, 2)),
             dma((fold, steps, 2)),
             pltpu.VMEM((rn // chans, steps, cr // 2, rd, ch), BF16),

time: 64.8 us -> 64.2 us (level)
  Pallas kernels: 62.3 us -> 61.4 us
    pallas_call x1, Pallas kernels: 62.3 us -> 61.4 us  [on_device(): pl.pallas_call(functools.partial(block_kernel, sizes), out_shape=jax.Shap...]
where the time goes in v4:
time: 64.2 us; the launch traced here: 63.7 us
  Pallas kernels  61.4 us (96%)
  local copies, waits for them, and re-layouts  2.26 us (4%)
    pallas_call x1, Pallas kernels, on_device(): pl.pallas_call(functools.partial(block_kernel, sizes), out_shape=jax.Shap...  61.4 us
    unnamed x1, local copies, waits for them, and re-layouts  2.26 us

profile of v4, /device:TPU:9, one launch (start us, length us, event | category | flops | bytes accessed | tf_op | source)
XLA Modules:
  0.0 63.7 jit_solution(10240152305677805878)
XLA Ops:
  0.0 61.4 %shard_map.109 = bf16[64,64,128]{2,1,0:T(8,128)(2,1)} custom-call(bf16[32,64,64]{2,1,0:T(8,128)(2,1)} %feat_ref.1, s32[32,64]{1,0:T(8,128)} %mask_ref.1, s32[1,256]{1,0:T(1,128)} %bitcast.7, bf16[32,64]{1,0:T(8,128)(2,1)} %bitcast.5, bf16[32,64]{1,0:T(8,128)(2,1)} %bitcast.6, bf16[64,64,128]{2,1,0:T(8,128)(2,1)} %rest_0_.1, bf16[1024,128]{1,0:T(8,128)(2,1)} %rest_1_.1, ...), custom_call_target="tpu_custom_call" | custom-call | tf_op jit(solution)/shard_map/pallas_call | solution.py:548
  61.4 2.3 %copy.13 = bf16[64,64,128]{2,1,0:T(8,128)(2,1)} copy(bf16[64,64,128]{2,1,0:T(8,128)(2,1)} %shard_map.109) | data formatting | bytes 2097152

commit v5 on v4

--- a/solution.py
+++ b/solution.py
@@ -128,9 +128,9 @@
     right = project(1, wr_ref)
     for k in range(fold):
         for g in range(lgroups):
-            lsend[k, g] = left[k * lgroups + g]
-        lsend[k, lgroups] = jnp.zeros((sl, 128), BF16)
-        lsend[k, lgroups, :, 0:rd] = mask[:, k * rd : (k + 1) * rd]
+            lsend[k, 1 + g] = left[k * lgroups + g]
+        lsend[k, 0] = jnp.zeros((sl, 128), BF16)
+        lsend[k, 0, :, 0:rd] = mask[:, k * rd : (k + 1) * rd]
     for g in range(rgroups):
         rg[row, g] = right[g]
     rg[row, rgroups] = jnp.zeros((sl, 128), BF16)
@@ -138,18 +138,46 @@
 
     pl.semaphore_wait(barrier, rn * cn)
 
-    for k in range(fold):
+    def span(n):
+        if isinstance(n, int) and n == 0:
+            return pl.ds(0, cgroups + 1)
+        return pl.ds(1 + n * cgroups, cgroups)
+
+    def l1_target(k):
         to_row, to_col = col * fold + k, row % cn
-        mine = jnp.logical_and(to_row == row, to_col == col)
-        slot = row // cn
-
-        @pl.when(mine)
-        def _():
-            pltpu.make_async_copy(lsend.at[k], lg.at[row], l1_recv.at[slot]).start()
-
-        @pl.when(jnp.logical_not(mine))
-        def _():
-            remote(lsend.at[k], lg.at[row], l1_send.at[k], l1_recv.at[slot], to_row, to_col).start()
+        return to_row, to_col, jnp.logical_and(to_row == row, to_col == col)
+
+    def send_left(n):
+        for k in range(fold):
+            to_row, to_col, mine = l1_target(k)
+            slot = row // cn
+            src, dst = lsend.at[k, span(n)], lg.at[row, span(n)]
+
+            @pl.when(mine)
+            def _():
+                pltpu.make_async_copy(src, dst, l1_recv.at[slot, n]).start()
+
+            @pl.when(jnp.logical_not(mine))
+            def _():
+                remote(src, dst, l1_send.at[k, n], l1_recv.at[slot, n], to_row, to_col).start()
+
+    def spread_left(n):
+        for m in range(fold):
+            piece = lg.at[col + m * cn, span(n)]
+            pltpu.make_async_copy(piece, piece, l1_recv.at[m, n]).wait()
+            for d in range(1, cn):
+                remote(
+                    piece, piece, l2_send.at[m, d - 1, n], l2_recv.at[m, d - 1, n],
+                    row, (col + d) % cn,
+                ).start()
+
+    def take_left(n):
+        for m in range(fold):
+            for d in range(1, cn):
+                piece = lg.at[(col + cn - d) % cn + m * cn, span(n)]
+                pltpu.make_async_copy(piece, piece, l2_recv.at[m, d - 1, n]).wait()
+
+    send_left(0)
 
     def chain(t):
         low, high = jnp.maximum(row - t, 0), jnp.minimum(row + t, rn - 1)
@@ -172,6 +200,8 @@
                     ).start()
 
     pass_on(0)
+    for n in range(1, steps):
+        send_left(n)
 
     tokens = valid_ref.shape[1]
     valid = valid_ref[...].astype(F32)
@@ -194,15 +224,7 @@
         for i in range(per):
             w4[q * 128 + i * pw : q * 128 + (i + 1) * pw, i * ch : (i + 1) * ch] = part
 
-    for m in range(fold):
-        slot = col + m * cn
-        pltpu.make_async_copy(lg.at[slot], lg.at[slot], l1_recv.at[m]).wait()
-        for d in range(1, cn):
-            remote(
-                lg.at[slot], lg.at[slot], l2_send.at[m, d - 1], l2_recv.at[m, d - 1],
-                row, (col + d) % cn,
-            ).start()
-
+    spread_left(0)
     for t in range(rn - 1):
         for e, piece in enumerate(pieces):
             for way, (there_is, slot) in enumerate((
@@ -226,21 +248,16 @@
                             to_row, col,
                         ).start()
 
+    for n in range(1, steps):
+        spread_left(n)
     for g in range(rgroups):
         slab = rg[:, g].astype(F32).reshape(depth, 128)
         rt[g * 128 : (g + 1) * 128, :] = slab.T
     for q in range(pw):
         rq[q * cd : (q + 1) * cd, :] = rt[pl.ds(q, cd, stride=pw), :].astype(BF16)
 
-    for m in range(fold):
-        for d in range(1, cn):
-            slot = (col + cn - d) % cn + m * cn
-            pltpu.make_async_copy(lg.at[slot], lg.at[slot], l2_recv.at[m, d - 1]).wait()
-    for g in range(lgroups):
-        slab = lg[:, g].astype(F32).reshape(depth, 128).astype(BF16)
-        where = g % cgroups
-        lcat[g // cgroups, :, where * 128 : (where + 1) * 128] = slab
-    left_mask = lg[:, lgroups].astype(F32).reshape(depth, 128)
+    take_left(0)
+    left_mask = lg[:, 0].astype(F32).reshape(depth, 128)
     right_mask = rg[:, rgroups].astype(F32).reshape(depth, 128)
     counts = dot(right_mask.T.astype(BF16), left_mask.astype(BF16))
     inverse = 1.0 / jnp.maximum(counts, 1.0)
@@ -313,7 +330,15 @@
     lag = min(1, steps)
 
     def one_step(step, carry):
-        lpart = lcat[step]
+
+        @pl.when(step > 0)
+        def _():
+            take_left(step)
+
+        for g in range(cgroups):
+            slab = lg[:, 1 + step * cgroups + g].astype(F32).reshape(depth, 128)
+            lcat[0, :, g * 128 : (g + 1) * 128] = slab.astype(BF16)
+        lpart = lcat[0]
         for q0 in range(0, pw, qstep):
             z = dot(rq[q0 * cd : (q0 + qstep) * cd, :], lpart).astype(BF16)
             for q in range(qstep):
@@ -470,11 +495,11 @@
     lax.fori_loop(0, rd // strip, conv, 0)
 
     for k in range(fold):
-        to_row, to_col = col * fold + k, row % cn
-
-        @pl.when(jnp.logical_not(jnp.logical_and(to_row == row, to_col == col)))
-        def _():
-            pltpu.make_async_copy(lsend.at[k], lsend.at[k], l1_send.at[k]).wait()
+        @pl.when(jnp.logical_not(l1_target(k)[2]))
+        def _():
+            for n in range(steps):
+                piece = lsend.at[k, span(n)]
+                pltpu.make_async_copy(piece, piece, l1_send.at[k, n]).wait()
 
         to_row, to_col = col * fold + k, row // fold
 
@@ -504,8 +529,9 @@
 
     for m in range(fold):
         for d in range(1, cn):
-            slot = col + m * cn
-            pltpu.make_async_copy(lg.at[slot], lg.at[slot], l2_send.at[m, d - 1]).wait()
+            for n in range(steps):
+                piece = lg.at[col + m * cn, span(n)]
+                pltpu.make_async_copy(piece, piece, l2_send.at[m, d - 1, n]).wait()
     for n, (a, b) in enumerate(AROUND):
 
         @pl.when(there(a, b))
@@ -560,7 +586,7 @@
             pltpu.VMEM((rn, cd // per + 1, sl, 128), BF16),
             pltpu.VMEM((cd * pw, depth), F32),
             pltpu.VMEM((pw * cd, depth), BF16),
-            pltpu.VMEM((steps, depth, cr * pw), BF16),
+            pltpu.VMEM((1, depth, cr * pw), BF16),
             pltpu.VMEM((pw * pw, ch), F32),
             pltpu.VMEM((pw * 128, per * ch), BF16),
             pltpu.VMEM((cr // per * cd, pw * 128), BF16),
@@ -574,10 +600,10 @@
             pltpu.VMEM((2, rd, ch), F32),
             pltpu.VMEM((8, tall, ch), BF16),
             pltpu.VMEM((8, tall, ch), BF16),
-            dma((fold,)),
-            dma((fold,)),
-            dma((fold, cn - 1)),
-            dma((fold, cn - 1)),
+            dma((fold, steps)),
+            dma((fold, steps)),
+            dma((fold, cn - 1, steps)),
+            dma((fold, cn - 1, steps)),
             dma((2, rn - 1, 2)),
             dma((rn, 2)),
             dma((fold, steps, 2)),

time: 64.2 us -> 64.1 us (level)
  no operation moved by 1% of the time
where the time goes in v5:
time: 64.1 us; the launch traced here: 63.6 us
  Pallas kernels  61.3 us (96%)
  local copies, waits for them, and re-layouts  2.26 us (4%)
    pallas_call x1, Pallas kernels, on_device(): pl.pallas_call(functools.partial(block_kernel, sizes), out_shape=jax.Shap...  61.3 us
    unnamed x1, local copies, waits for them, and re-layouts  2.26 us

profile of v5, /device:TPU:9, one launch (start us, length us, event | category | flops | bytes accessed | tf_op | source)
XLA Modules:
  0.0 63.6 jit_solution(1320436460327045423)
XLA Ops:
  0.0 61.3 %shard_map.109 = bf16[64,64,128]{2,1,0:T(8,128)(2,1)} custom-call(bf16[32,64,64]{2,1,0:T(8,128)(2,1)} %feat_ref.1, s32[32,64]{1,0:T(8,128)} %mask_ref.1, s32[1,256]{1,0:T(1,128)} %bitcast.7, bf16[32,64]{1,0:T(8,128)(2,1)} %bitcast.5, bf16[32,64]{1,0:T(8,128)(2,1)} %bitcast.6, bf16[64,64,128]{2,1,0:T(8,128)(2,1)} %rest_0_.1, bf16[1024,128]{1,0:T(8,128)(2,1)} %rest_1_.1, ...), custom_call_target="tpu_custom_call" | custom-call | tf_op jit(solution)/shard_map/pallas_call | solution.py:574
  61.3 2.3 %copy.13 = bf16[64,64,128]{2,1,0:T(8,128)(2,1)} copy(bf16[64,64,128]{2,1,0:T(8,128)(2,1)} %shard_map.109) | data formatting | bytes 2097152
